TPU v7x, 128 devices: a whole 4x4x4 slice. The times are simulated.
128 devices in a mesh: req: 8 (over z, core), seq: 16 (over x, y).
Axes of the slice: x: 4, y: 4, z: 4, core: 2. Of those that a mesh axis runs over, the one named last changes fastest.
Arguments:
- token_ids: int32 [64, 4], replicated, may hold values from 0 to 127999, as said below
- embed_table: bfloat16 [128000, 1024], P(('req', 'seq')), may hold values from -6 to 6
- ln_gains: float32 [4, 1024], replicated, may hold values from 0.25 to 1.75
- ln_biases: float32 [4, 1024], replicated, may hold values from -1.5 to 1.5
- rel_table: bfloat16 [512, 1024], replicated, may hold values from -6 to 6
- w_qkv: bfloat16 [1024, 3072], replicated, may hold values from -0.1875 to 0.1875
- w_out: bfloat16 [1024, 1024], replicated, may hold values from -0.1875 to 0.1875
- cache_keys: bfloat16 [64, 8192, 1024], P('req', 'seq'), may hold values from -3000 to 3000
- cache_values: bfloat16 [64, 8192, 1024], P('req', 'seq'), may hold values from -6 to 6
- lengths: int32 [64], P('req'), may hold values from 129 to 8192, as said below
- window_starts: int32 [64], P('req'), may hold values from 4 to 4096, as said below
- cache_buckets: int32 [64, 4, 8192], P('req', None, 'seq'), may hold values from 0 to 511
- new_buckets: int32 [64, 4, 4], P('req'), may hold values from 0 to 511
- w_in: bfloat16 [4096, 1024], P('seq'), may hold values from -0.1875 to 0.1875
- w_down: bfloat16 [4096, 1024], P('seq'), may hold values from -0.09375 to 0.09375
Outputs:
- layer_out: bfloat16 [64, 4, 1024], P('req')
Inputs may be any that keep to these rules, and one draw needn't show every extreme that they name: `token_ids`: every aligned block of 1000 ids holds the id of at least one new token. `lengths`: some request has length 8192. window_starts = max(4, lengths - 4096) for each request.
All inputs are finite; a program needn't handle non-finite values.
Results may differ from a plain program's by a relative error of at most 0.018.
Values may be sent and summed in bfloat16 or wider, within the bound.
A program may use at most 192 MiB of HBM per device.

v0:
```python
import math

import jax
import jax.numpy as jnp
from jax import lax
from jax.sharding import PartitionSpec as P

HEADS = 16
HEAD_DIM = 64
SINKS = 4


norm_epsilon = 1e-06
masked_score = -1e30


def layer_norm(values, gain, shift):
    center = values - jnp.mean(values, axis=-1, keepdims=True)
    spread = jnp.mean(center * center, axis=-1, keepdims=True)
    return center * lax.rsqrt(spread + norm_epsilon) * gain + shift


def expand_rows(rows_x, in_rows, down_rows):
    inner = lax.dot_general(
        rows_x, in_rows, (((1,), (1,)), ((), ())), preferred_element_type=jnp.float32
    )
    inner = jax.nn.gelu(inner, approximate=False).astype(jnp.bfloat16)
    return jnp.dot(inner, down_rows, preferred_element_type=jnp.float32)


def shards(
    token_ids,
    embed_table,
    ln_gains,
    ln_biases,
    rel_table,
    w_qkv,
    w_out,
    cache_keys,
    cache_values,
    lengths,
    window_starts,
    cache_buckets,
    new_buckets,
    w_in,
    w_down,
):
    group_reqs, piece_len, width = cache_keys.shape
    new_count = token_ids.shape[1]
    vocab_rows = embed_table.shape[0]
    bucket_count = rel_table.shape[0]
    group_rows = group_reqs * new_count
    seq_index = lax.axis_index("seq")
    req_index = lax.axis_index("req")
    owner_index = req_index * lax.axis_size("seq") + seq_index
    local_ids = token_ids.reshape(-1) - owner_index * vocab_rows
    one_hot = (local_ids[:, None] == jnp.arange(vocab_rows, dtype=jnp.int32)[None, :]).astype(
        jnp.bfloat16
    )
    looked_up = jnp.dot(one_hot, embed_table, preferred_element_type=jnp.float32)
    summed = lax.psum(looked_up, ("req", "seq"))
    own_rows = lax.dynamic_slice_in_dim(summed, req_index * group_rows, group_rows, 0)
    hidden_zero = layer_norm(own_rows, ln_gains[0], ln_biases[0]).astype(jnp.bfloat16)
    relative = layer_norm(rel_table.astype(jnp.float32), ln_gains[3], ln_biases[3]).astype(
        jnp.bfloat16
    )
    pos_query = jnp.dot(relative, w_qkv[:, :width], preferred_element_type=jnp.float32).astype(
        jnp.bfloat16
    )
    pos_key = jnp.dot(
        relative, w_qkv[:, width : 2 * width], preferred_element_type=jnp.float32
    ).astype(jnp.bfloat16)
    projected = jnp.dot(hidden_zero, w_qkv, preferred_element_type=jnp.float32).astype(jnp.bfloat16)
    queries = projected[:, :width].reshape(group_reqs, new_count, HEADS, HEAD_DIM)
    fresh_keys = projected[:, width : 2 * width].reshape(group_reqs, new_count, HEADS, HEAD_DIM)
    fresh_values = projected[:, 2 * width :].reshape(group_reqs, new_count, HEADS, HEAD_DIM)
    pos_key_heads = pos_key.reshape(bucket_count, HEADS, HEAD_DIM)
    reversed_query_heads = pos_query[::-1].reshape(bucket_count, HEADS, HEAD_DIM)
    query_table = jnp.einsum(
        "rthd,bhd->rhtb", queries, pos_key_heads, preferred_element_type=jnp.float32
    )
    score_scale = 1.0 / math.sqrt(3 * HEAD_DIM)
    bucket_range = jnp.arange(bucket_count, dtype=jnp.int32)
    first_place = seq_index * piece_len
    positions = first_place + jnp.arange(piece_len, dtype=jnp.int32)
    piece_live = (first_place < lengths) & (
        (first_place < SINKS) | (first_place + piece_len > window_starts)
    )
    key_heads = cache_keys.reshape(group_reqs, piece_len, HEADS, HEAD_DIM)
    value_heads = cache_values.reshape(group_reqs, piece_len, HEADS, HEAD_DIM)

    def piece_scores(queries_one, table_one, keys_one, buckets_one, length_one, start_one):
        content = jnp.einsum(
            "thd,phd->htp", queries_one, keys_one, preferred_element_type=jnp.float32
        )
        selector = (buckets_one[:, :, None] == bucket_range[None, None, :]).astype(jnp.float32)
        to_pos = jnp.einsum("tpb,htb->htp", selector, table_one, precision=lax.Precision.HIGHEST)
        key_table = jnp.einsum(
            "phd,bhd->hpb", keys_one, reversed_query_heads, preferred_element_type=jnp.float32
        )
        from_pos = jnp.einsum("tpb,hpb->htp", selector, key_table, precision=lax.Precision.HIGHEST)
        allowed = (positions < length_one) & ((positions < SINKS) | (positions >= start_one))
        return jnp.where(
            allowed[None, None, :], (content + to_pos + from_pos) * score_scale, masked_score
        )

    def score_step(items):
        queries_one, table_one, keys_one, buckets_one, length_one, start_one, live_one = items
        return piece_scores(queries_one, table_one, keys_one, buckets_one, length_one, start_one)

    scores = lax.map(
        score_step,
        (queries, query_table, key_heads, cache_buckets, lengths, window_starts, piece_live),
    )
    content_new = jnp.einsum(
        "rthd,ruhd->rhtu", queries, fresh_keys, preferred_element_type=jnp.float32
    )
    to_pos_new = jnp.take_along_axis(
        query_table,
        jnp.broadcast_to(new_buckets[:, None], (group_reqs, HEADS, new_count, new_count)),
        axis=3,
    )
    gathered_new = jnp.take(pos_query, bucket_count - 1 - new_buckets, axis=0).reshape(
        group_reqs, new_count, new_count, HEADS, HEAD_DIM
    )
    from_pos_new = jnp.einsum(
        "rtuhd,ruhd->rhtu", gathered_new, fresh_keys, preferred_element_type=jnp.float32
    )
    causal = jnp.arange(new_count)[None, :] <= jnp.arange(new_count)[:, None]
    fresh_scores = jnp.where(
        causal, (content_new + to_pos_new + from_pos_new) * score_scale, masked_score
    )
    row_max = jnp.maximum(lax.pmax(jnp.max(scores, axis=-1), "seq"), jnp.max(fresh_scores, axis=-1))

    def weigh_piece(scores_one, max_one, values_one):
        exp_terms = jnp.exp(scores_one - max_one[:, :, None])
        numerator = jnp.einsum(
            "htp,phd->thd",
            exp_terms.astype(jnp.bfloat16),
            values_one,
            preferred_element_type=jnp.float32,
        )
        return (numerator, jnp.sum(exp_terms, axis=-1))

    def weigh_step(items):
        scores_one, max_one, values_one, live_one = items
        return weigh_piece(scores_one, max_one, values_one)

    numerators, denominators = lax.map(weigh_step, (scores, row_max, value_heads, piece_live))
    numer_total, denom_total = lax.psum((numerators, denominators), "seq")
    fresh_exp = jnp.exp(fresh_scores - row_max[..., None])
    fresh_numer = jnp.einsum(
        "rhtu,ruhd->rthd",
        fresh_exp.astype(jnp.bfloat16),
        fresh_values,
        preferred_element_type=jnp.float32,
    )
    denom_all = jnp.transpose(denom_total + jnp.sum(fresh_exp, axis=-1), (0, 2, 1))
    attended = (
        ((numer_total + fresh_numer) / denom_all[..., None])
        .astype(jnp.bfloat16)
        .reshape(group_rows, width)
    )
    attn_out = jnp.dot(attended, w_out, preferred_element_type=jnp.float32)
    hidden_one = layer_norm(
        hidden_zero.astype(jnp.float32) + attn_out, ln_gains[1], ln_biases[1]
    ).astype(jnp.bfloat16)
    partial_mlp = expand_rows(hidden_one, w_in, w_down)
    mlp_out = lax.psum(partial_mlp.astype(jnp.bfloat16), "seq").astype(jnp.float32)
    layer_out = layer_norm(
        hidden_one.astype(jnp.float32) + mlp_out, ln_gains[2], ln_biases[2]
    ).astype(jnp.bfloat16)
    return layer_out.reshape(group_reqs, new_count, width)


def solution(mesh):
    in_specs = (
        P(),
        P(("req", "seq"), None),
        P(),
        P(),
        P(),
        P(),
        P(),
        P("req", "seq", None),
        P("req", "seq", None),
        P("req"),
        P("req"),
        P("req", None, "seq"),
        P("req", None, None),
        P("seq", None),
        P("seq", None),
    )
    out_specs = P("req", None, None)
    return jax.shard_map(shards, mesh=mesh, in_specs=in_specs, out_specs=out_specs, check_vma=False)
```

profile of v0, /device:TPU:0, one launch (start us, length us, event | category | flops | bytes accessed | tf_op | source)
XLA Modules:
  0.0 749.9 jit_solution(12523177118049195866)
XLA Ops:
  7.6 3.4 fusion.55
  13.0 2.9 fusion.49
  16.0 3.9 fusion.46
  20.9 10.3 %rev.3 = bf16[512,1024]{1,0:T(8,128)(2,1)} reverse(bf16[512,1024]{1,0:T(8,128)(2,1)S(1)} %fusion.49), dimensions={0} | reverse | bytes 2097152 | tf_op jit(solution)/shard_map/rev | solution.py:78
  32.1 2.3 copy.113
  34.7 2.3 copy.111
  37.0 11.4 %copy.110 = bf16[8,512,1024]{1,2,0:T(8,128)(2,1)} copy(bf16[8,512,1024]{2,1,0:T(8,128)(2,1)} %param.26) | data formatting | bytes 16777216 | tf_op args[7]
  48.5 11.4 %copy.109 = bf16[8,512,1024]{1,2,0:T(8,128)(2,1)} copy(bf16[8,512,1024]{2,1,0:T(8,128)(2,1)} %param.27) | data formatting | bytes 16777216 | tf_op args[8]
  60.6 100.8 %all-reduce.4.cloned.1.call-done = f32[256,1024]{1,0:T(8,128)} async-done(((f32[256,1024]{1,0:T(8,128)}), f32[256,1024]{1,0:T(8,128)}) %all-reduce.4.cloned.1.call-update) | async-done | bytes 1048592 | tf_op jit(solution)/shard_map/psum | solution.py:61
  163.6 4.1 convolution_convert_fusion
  172.7 19.5 %gather_fusion.1 = f32[2048]{0:T(1024)S(1)} fusion(f32[8,16,4,512]{3,0,2,1:T(8,128)S(1)} %convolution_bitcast_fusion.1, s32[2048]{0:T(1024)S(1)} %reshape.131), kind=kCustom, calls=%fused_computation.1 | custom fusion | bytes 49152 | tf_op jit(solution)/shard_map/jit(take_along_axis)/gather | solution.py:118
  195.7 272.9 %while.24 = (s32[]{:T(128)}, f32[8,16,4,512]{3,2,1,0:T(4,128)}, s32[8]{0:T(128)}, s32[8]{0:T(128)}, bf16[8,4,16,64]{3,1,2,0:T(4,128)(2,1)}, /*index=5*/bf16[8,51...) while((s32[]{:T(128)}, f32[8,16,4,512]{3,2,1,0:T(4,128)}, ...), condition=%wide.region_6.7_spmd.clone, body=%wide.region_5.6_spmd.clone.sunk | while | flops 945949696 | bytes 44370624 | solution.py:111
  202.8 2.6 fusion.190
  205.4 3.6 fusion.188
  209.0 17.1 %fusion.189 = f32[512,16,4]{1,2,0:T(4,128)} fusion(f32[16,512,512]{2,1,0:T(8,128)S(1)} %fusion.188, s32[4,512]{0,1:T(8,128)S(1)} %bitcast.130), kind=kOutput, calls=%fused_computation.16.clone.1 | convolution fusion | flops 202375168 | bytes 16916480 | tf_op jit(solution)/shard_map/while/body/eval_jaxpr/tpb,hpb->htp/dot_general | solution.py:101
  236.9 2.6 fusion.190
  239.5 3.6 fusion.188
  243.1 17.1 %fusion.189 = f32[512,16,4]{1,2,0:T(4,128)} fusion(f32[16,512,512]{2,1,0:T(8,128)S(1)} %fusion.188, s32[4,512]{0,1:T(8,128)S(1)} %bitcast.130), kind=kOutput, calls=%fused_computation.16.clone.1 | convolution fusion | flops 202375168 | bytes 16916480 | tf_op jit(solution)/shard_map/while/body/eval_jaxpr/tpb,hpb->htp/dot_general | solution.py:101
  271.0 2.6 fusion.190
  273.6 3.6 fusion.188
  277.3 17.1 %fusion.189 = f32[512,16,4]{1,2,0:T(4,128)} fusion(f32[16,512,512]{2,1,0:T(8,128)S(1)} %fusion.188, s32[4,512]{0,1:T(8,128)S(1)} %bitcast.130), kind=kOutput, calls=%fused_computation.16.clone.1 | convolution fusion | flops 202375168 | bytes 16916480 | tf_op jit(solution)/shard_map/while/body/eval_jaxpr/tpb,hpb->htp/dot_general | solution.py:101
  305.1 2.6 fusion.190
  307.8 3.6 fusion.188
  311.4 17.1 %fusion.189 = f32[512,16,4]{1,2,0:T(4,128)} fusion(f32[16,512,512]{2,1,0:T(8,128)S(1)} %fusion.188, s32[4,512]{0,1:T(8,128)S(1)} %bitcast.130), kind=kOutput, calls=%fused_computation.16.clone.1 | convolution fusion | flops 202375168 | bytes 16916480 | tf_op jit(solution)/shard_map/while/body/eval_jaxpr/tpb,hpb->htp/dot_general | solution.py:101
  339.2 2.6 fusion.190
  341.9 3.6 fusion.188
  345.5 17.1 %fusion.189 = f32[512,16,4]{1,2,0:T(4,128)} fusion(f32[16,512,512]{2,1,0:T(8,128)S(1)} %fusion.188, s32[4,512]{0,1:T(8,128)S(1)} %bitcast.130), kind=kOutput, calls=%fused_computation.16.clone.1 | convolution fusion | flops 202375168 | bytes 16916480 | tf_op jit(solution)/shard_map/while/body/eval_jaxpr/tpb,hpb->htp/dot_general | solution.py:101
  373.4 2.6 fusion.190
  376.0 3.6 fusion.188
  379.6 17.1 %fusion.189 = f32[512,16,4]{1,2,0:T(4,128)} fusion(f32[16,512,512]{2,1,0:T(8,128)S(1)} %fusion.188, s32[4,512]{0,1:T(8,128)S(1)} %bitcast.130), kind=kOutput, calls=%fused_computation.16.clone.1 | convolution fusion | flops 202375168 | bytes 16916480 | tf_op jit(solution)/shard_map/while/body/eval_jaxpr/tpb,hpb->htp/dot_general | solution.py:101
  407.5 2.6 fusion.190
  410.1 3.6 fusion.188
  413.7 17.1 %fusion.189 = f32[512,16,4]{1,2,0:T(4,128)} fusion(f32[16,512,512]{2,1,0:T(8,128)S(1)} %fusion.188, s32[4,512]{0,1:T(8,128)S(1)} %bitcast.130), kind=kOutput, calls=%fused_computation.16.clone.1 | convolution fusion | flops 202375168 | bytes 16916480 | tf_op jit(solution)/shard_map/while/body/eval_jaxpr/tpb,hpb->htp/dot_general | solution.py:101
  441.6 2.6 fusion.190
  444.2 3.6 fusion.188
  447.8 17.1 %fusion.189 = f32[512,16,4]{1,2,0:T(4,128)} fusion(f32[16,512,512]{2,1,0:T(8,128)S(1)} %fusion.188, s32[4,512]{0,1:T(8,128)S(1)} %bitcast.130), kind=kOutput, calls=%fused_computation.16.clone.1 | convolution fusion | flops 202375168 | bytes 16916480 | tf_op jit(solution)/shard_map/while/body/eval_jaxpr/tpb,hpb->htp/dot_general | solution.py:101
  470.1 73.2 %pmax.7 = f32[8,16,4]{2,1,0:T(8,128)S(1)} all-reduce(f32[8,16,4]{2,1,0:T(8,128)S(1)} %reduce_max.18), channel_id=1, replica_groups=mesh['req'=8,'seq'=16] {'seq'}, use_global_device_ids=true, to_apply=%region_8.9 | all-reduce | flops 512 | bytes 4096 | tf_op jit(solution)/shard_map/pmax | solution.py:133
  546.8 28.4 %while.23 = (s32[]{:T(128)}, f32[8,4,16,64]{3,1,2,0:T(4,128)}, f32[8,16,4]{1,2,0:T(4,128)S(1)}, bf16[8,512,16,64]{1,3,2,0:T(8,128)(2,1)}, f32[8,16,4,512]{3,2,1,0:T(4,128)}, /*index=5*/f32[8,16,4]{1,2,0:T(4,128)S(1)}, s32[]{:T(128)}) while((s32[]{:T(128)}, f32[8,4,16,64]{3,1,2,0:T(4,128)}, f32[8,16,4]{1,2,0:T(4,128)S(1)}, ...), condition=%wide.region_12.13_spmd, body=%wide.region_10.12_spmd.sunk | while | flops 4325314 | bytes 1351521 | solution.py:149
  548.1 2.3 fusion.180
  551.6 2.3 fusion.180
  558.7 2.3 fusion.180
  562.3 2.3 fusion.180
  565.8 2.3 fusion.180
  572.9 2.3 fusion.180
  575.4 69.6 %psum.30 = f32[8,16,4]{2,1,0:T(8,128)S(1)} all-reduce(f32[8,16,4]{2,1,0:T(8,128)S(1)} %copy.129), channel_id=1, replica_groups=mesh['req'=8,'seq'=16] {'seq'}, use_global_device_ids=true, to_apply=%region_14.15 | all-reduce | flops 512 | bytes 4096 | tf_op jit(solution)/shard_map/psum | solution.py:150
  645.0 8.7 %all-reduce.6.cloned.1.call-done = f32[8,4,16,64]{3,1,2,0:T(4,128)} async-done(((f32[8,4,16,64]{3,1,2,0:T(4,128)}), f32[8,4,16,64]{3,1,2,0:T(4,128)}) %all-reduce.6.cloned.1.call-update) | async-done | bytes 131088 | tf_op jit(solution)/shard_map/psum | solution.py:150
  657.0 2.3 convolution_convert_fusion.1
  659.3 80.3 %all-reduce.8.cloned.1.call-done = bf16[32,1024]{1,0:T(8,128)(2,1)} async-done(((bf16[32,1024]{1,0:T(8,128)(2,1)}), bf16[32,1024]{1,0:T(8,128)(2,1)}) %all-reduce.8.cloned.1.call-update) | async-done | bytes 65552 | tf_op jit(solution)/shard_map/psum | solution.py:169
  (246 shorter events, 128.7 us)
Async XLA Ops:
  6.5 648.7 %copy-start = (bf16[1024,1024]{1,0:T(8,128)(2,1)S(1)}, bf16[1024,1024]{1,0:T(8,128)(2,1)}, u32[]{:S(2)}) copy-start(bf16[1024,1024]{1,0:T(8,128)(2,1)} %param.25) | copy-start | bytes 6291460
  6.5 154.9 %all-reduce.4.cloned.1.call-start = ((), (), s32[]{:S(2)}) async-start(), calls=%async_computation | async-start | bytes 2097152 | tf_op jit(solution)/shard_map/psum | solution.py:61
  7.6 3.5 copy-start.4
  7.6 3.6 copy-start.2
  11.0 0.8 copy-start.16
  11.0 1.4 copy-start.17
  11.0 642.7 %all-reduce.6.cloned.1.call-start = ((), (), s32[]{:S(2)}) async-start(), calls=%async_computation.1 | async-start | bytes 524288 | tf_op jit(solution)/shard_map/psum | solution.py:150
  11.1 2.0 copy-start.3
  11.1 8.8 %copy-start.12 = (pred[8,4,4]{0,2,1:T(4,128)(4,1)}, pred[8,4,4]{0,2,1:T(4,128)(4,1)S(1)}, u32[]{:S(2)}) copy-start(pred[8,4,4]{0,2,1:T(4,128)(4,1)S(1)} %get-tuple-element.221) | copy-start | bytes 388
  11.2 8.7 %copy-start.5 = (s32[8,4,4]{0,2,1:T(4,128)}, s32[8,4,4]{0,2,1:T(4,128)S(1)}, u32[]{:S(2)}) copy-start(s32[8,4,4]{0,2,1:T(4,128)S(1)} %get-tuple-element.223) | copy-start | bytes 1540
  12.4 151.1 %copy-start.8 = (f32[1,1024]{1,0:T(1,128)}, f32[1,1024]{1,0:T(1,128)S(1)}, u32[]{:S(2)}) copy-start(f32[1,1024]{1,0:T(1,128)S(1)} %get-tuple-element.215) | copy-start | bytes 12292
  13.0 150.5 %copy-start.10 = (f32[1,1024]{1,0:T(1,128)}, f32[1,1024]{1,0:T(1,128)S(1)}, u32[]{:S(2)}) copy-start(f32[1,1024]{1,0:T(1,128)S(1)} %get-tuple-element.219) | copy-start | bytes 12292
  162.4 5.3 copy-start.18
  163.6 4.2 copy-start.20
  201.1 4.3 copy-start.1
  235.2 4.3 copy-start.1
  269.4 4.3 copy-start.1
  303.5 4.3 copy-start.1
  337.6 4.3 copy-start.1
  371.7 4.3 copy-start.1
  405.8 4.3 copy-start.1
  440.0 4.3 copy-start.1
  468.7 78.1 %copy-start.15 = (f32[8,16,4]{1,2,0:T(4,128)S(1)}, f32[8,16,4]{1,2,0:T(4,128)}, u32[]{:S(2)}) copy-start(f32[8,16,4]{1,2,0:T(4,128)} %custom-call.5) | copy-start | bytes 6148
  575.2 80.0 %copy-start.9 = (f32[1,1024]{1,0:T(1,128)S(1)}, f32[1,1024]{1,0:T(1,128)}, u32[]{:S(2)}) copy-start(f32[1,1024]{1,0:T(1,128)} %copy-done.8) | copy-start | bytes 12292
  575.2 80.0 %copy-start.11 = (f32[1,1024]{1,0:T(1,128)S(1)}, f32[1,1024]{1,0:T(1,128)}, u32[]{:S(2)}) copy-start(f32[1,1024]{1,0:T(1,128)} %copy-done.10) | copy-start | bytes 12292
  575.2 80.0 %copy-start.19 = (f32[32]{0:T(128)S(1)}, f32[32]{0:T(128)}, u32[]{:S(2)}) copy-start(f32[32]{0:T(128)} %copy-done.18) | copy-start | bytes 388
  575.2 80.0 %copy-start.21 = (f32[32]{0:T(128)S(1)}, f32[32]{0:T(128)}, u32[]{:S(2)}) copy-start(f32[32]{0:T(128)} %copy-done.20) | copy-start | bytes 388
  575.2 164.4 %all-reduce.8.cloned.1.call-start = ((), (), s32[]{:S(2)}) async-start(), calls=%async_computation.2 | async-start | bytes 131072 | tf_op jit(solution)/shard_map/psum | solution.py:169
  655.0 2.0 copy-start.6
  655.0 2.0 copy-start.7
  655.0 2.0 copy-start.22
  655.2 86.5 %copy-start.13 = (f32[1,1024]{1,0:T(1,128)S(1)}, f32[1,1024]{1,0:T(1,128)}, u32[]{:S(2)}) copy-start(f32[1,1024]{1,0:T(1,128)} %get-tuple-element.213) | copy-start | bytes 12292
  655.3 86.5 %copy-start.14 = (f32[1,1024]{1,0:T(1,128)S(1)}, f32[1,1024]{1,0:T(1,128)}, u32[]{:S(2)}) copy-start(f32[1,1024]{1,0:T(1,128)} %get-tuple-element.217) | copy-start | bytes 12292
Sparse Core Ops, SparseCore 0:
  12.2 149.2 all-reduce.3
  575.4 78.3 all-reduce.5
  659.4 80.1 all-reduce.7
where the time goes:
time: 753 us; the launch traced here: 750 us
  matrix products  244 us (32%)
  waiting for transfers between devices  190 us (25%)
  blocking collectives  143 us (19%)
  local copies, waits for them, and re-layouts  115 us (15%)
  other arithmetic  44.1 us (6%)
  between operations  13.6 us (2%)
    dot_general x8, matrix products, piece_scores(): jnp.einsum('tpb,hpb->htp', selector, key_table, precision=lax.Precision.H...  137 us
    psum x1, waiting for transfers between devices, shards(): summed = lax.psum(looked_up, ('req', 'seq'))  101 us
    psum x1, waiting for transfers between devices, shards(): lax.psum(partial_mlp.astype(jnp.bfloat16), 'seq').astype(jnp.float32)  80.3 us
    pmax x1, blocking collectives, shards(): lax.pmax(jnp.max(scores, axis=-1), 'seq')  73.2 us
    psum x1, blocking collectives, shards(): numer_total, denom_total = lax.psum((numerators, denominators), 'seq')  69.6 us
    dynamic_slice x40, local copies, waits for them, and re-layouts, shards(): lax.map(score_step, (queries, query_table, key_heads, cache_buckets, leng...  33.2 us
    dot_general x8, matrix products, piece_scores(): jnp.einsum('phd,bhd->hpb', keys_one, reversed_query_heads, preferred_elem...  28.9 us
    unnamed x49, local copies, waits for them, and re-layouts  24.5 us
  transfers between devices with their start and end apart: 3, of which 3 were waited for; matrix products, arithmetic and copies ran while one was open for 7% of the time, Pallas kernels for 0%

commit v1 on v0

v1 whole, which is shorter than its diff:
```python
import functools
import math

import jax
import jax.numpy as jnp
from jax import lax
from jax.experimental import pallas as pl
from jax.experimental.pallas import tpu as pltpu
from jax.sharding import PartitionSpec as P

HEADS = 16
HEAD_DIM = 64
SINKS = 4
NEW = 4
WIDTH = 1024
REQ_N = 8
SEQ_N = 16
GROUP = 8
ROWS = GROUP * NEW
PIECE = 512
BUCKETS = 512
TILE = 256
LANES = 128
CHUNKS = WIDTH // LANES
MSG = 24

norm_epsilon = 1e-06
masked_score = -1e30
score_scale = 1.0 / math.sqrt(3 * HEAD_DIM)
MESH = pl.DeviceIdType.MESH
f32 = jnp.float32
bf16 = jnp.bfloat16


def layer_norm(values, gain, shift):
    center = values - jnp.mean(values, axis=-1, keepdims=True)
    spread = jnp.mean(center * center, axis=-1, keepdims=True)
    return center * lax.rsqrt(spread + norm_epsilon) * gain + shift


def dot_nt(a, b):
    return lax.dot_general(a, b, (((1,), (1,)), ((), ())), preferred_element_type=f32)


def rows_to_tiles(rows, stage, count):
    for c in range(CHUNKS):
        stage[pl.ds(c, count, stride=CHUNKS), :] = rows[:, c * LANES : (c + 1) * LANES]


def tiles_to_rows(stage, count):
    return jnp.concatenate(
        [stage[pl.ds(c, count, stride=CHUNKS), :] for c in range(CHUNKS)], axis=1
    )


def seq_copy(src, dst, send_sem, recv_sem, peer):
    return pltpu.make_async_remote_copy(
        src_ref=src,
        dst_ref=dst,
        send_sem=send_sem,
        recv_sem=recv_sem,
        device_id={"seq": peer},
        device_id_type=MESH,
    )


def seq_scatter(me, send, recv, send_sems, recv_sems):
    copies = []
    for k in range(1, SEQ_N):
        peer = lax.rem(me + k, SEQ_N)
        copy = seq_copy(send.at[peer], recv.at[k], send_sems.at[k], recv_sems.at[k], peer)
        copy.start()
        copies.append(copy)
    return copies


def seq_gather(me, buf, send_sems, recv_sems):
    copies = []
    for k in range(1, SEQ_N):
        peer = lax.rem(me + k, SEQ_N)
        copy = seq_copy(buf.at[me], buf.at[me], send_sems.at[k], recv_sems.at[k], peer)
        copy.start()
        copies.append(copy)
    return copies


def wait_all(copies):
    for copy in copies:
        copy.wait()


def embed_kernel(
    ids_ref, table_ref, gain_ref, bias_ref, out_ref, send, land, stage, tiles, got, hid, rows_f,
    req_send, req_recv, rs_send, rs_recv, ag_send, ag_recv,
):
    me = lax.axis_index("seq")
    req = lax.axis_index("req")
    barrier = pltpu.get_barrier_semaphore()
    for k in range(1, SEQ_N):
        pl.semaphore_signal(
            barrier, inc=1, device_id={"seq": lax.rem(me + k, SEQ_N)}, device_id_type=MESH
        )
    for k in range(1, REQ_N):
        pl.semaphore_signal(
            barrier, inc=1, device_id={"req": lax.rem(req + k, REQ_N)}, device_id_type=MESH
        )
    vocab_rows = table_ref.shape[0]
    local = ids_ref[...] - (req * SEQ_N + me) * vocab_rows
    one_hot = (
        lax.broadcasted_iota(jnp.int32, (REQ_N * ROWS, vocab_rows), 1) == local
    ).astype(f32).astype(bf16)
    send[...] = (
        jnp.dot(one_hot, table_ref[...], preferred_element_type=f32)
        .astype(bf16)
        .reshape(REQ_N, ROWS, WIDTH)
    )
    pl.semaphore_wait(barrier, SEQ_N - 1 + REQ_N - 1)
    copies = []
    for k in range(1, REQ_N):
        peer = lax.rem(req + k, REQ_N)
        copy = pltpu.make_async_remote_copy(
            src_ref=send.at[peer],
            dst_ref=land.at[k],
            send_sem=req_send.at[k],
            recv_sem=req_recv.at[k],
            device_id={"req": peer},
            device_id_type=MESH,
        )
        copy.start()
        copies.append(copy)
    total = send[req].astype(f32)
    for k in range(1, REQ_N):
        copies[k - 1].wait()
        total = total + land[k].astype(f32)
    rows_to_tiles(total, stage, ROWS)
    tiles[...] = stage[...].reshape(SEQ_N, 2 * CHUNKS, LANES).astype(bf16)
    copies = seq_scatter(me, tiles, got, rs_send, rs_recv)
    own = tiles[me].astype(f32)
    for k in range(1, SEQ_N):
        copies[k - 1].wait()
        own = own + got[k].astype(f32)
    rows_f[...] = own
    hidden = layer_norm(tiles_to_rows(rows_f, 2), gain_ref[0:1, :], bias_ref[0:1, :])
    rows_to_tiles(hidden, rows_f, 2)
    hid[me] = rows_f[...].astype(bf16)
    wait_all(seq_gather(me, hid, ag_send, ag_recv))
    stage[...] = hid[...].astype(f32).reshape(ROWS * CHUNKS, LANES)
    out_ref[...] = tiles_to_rows(stage, ROWS).astype(bf16)


def embed_call(ids, table, gains, biases):
    slot = (SEQ_N, 2 * CHUNKS, LANES)
    return pl.pallas_call(
        embed_kernel,
        out_shape=jax.ShapeDtypeStruct((ROWS, WIDTH), bf16),
        in_specs=[pl.BlockSpec(memory_space=pltpu.VMEM)] * 4,
        out_specs=pl.BlockSpec(memory_space=pltpu.VMEM),
        scratch_shapes=[
            pltpu.VMEM((REQ_N, ROWS, WIDTH), bf16),
            pltpu.VMEM((REQ_N, ROWS, WIDTH), bf16),
            pltpu.VMEM((ROWS * CHUNKS, LANES), f32),
            pltpu.VMEM(slot, bf16),
            pltpu.VMEM(slot, bf16),
            pltpu.VMEM(slot, bf16),
            pltpu.VMEM((2 * CHUNKS, LANES), f32),
        ]
        + [pltpu.SemaphoreType.DMA((REQ_N,))] * 2
        + [pltpu.SemaphoreType.DMA((SEQ_N,))] * 4,
        compiler_params=pltpu.CompilerParams(
            collective_id=0, has_side_effects=True, vmem_limit_bytes=32 << 20
        ),
        name="embed_exchange",
    )(ids, table, gains, biases)


def spread_pair(column_even, column_odd, lane):
    return jnp.where(lane < HEAD_DIM, column_even, column_odd)


def pack_ml(values, lane):
    out = jnp.zeros((CHUNKS, LANES), f32)
    for g, value in enumerate(values):
        out = jnp.where((lane >> 4) == g, value, out)
    return out


def attend_kernel(
    lengths_ref, starts_ref, place_ref,
    hidden_ref, rel_ref, gain_ref, bias_ref, w_ref, keys_ref, values_ref, buckets_ref, new_ref,
    msg_ref, fresh_ref,
    proj, pos_lhs, pos_key, keys_t, from_pos, stage, fresh_stage,
):
    r = pl.program_id(0)
    lane = lax.broadcasted_iota(jnp.int32, (CHUNKS, LANES), 1)
    table_rows = NEW * HEADS

    @pl.when(r == 0)
    def _():
        relative = layer_norm(rel_ref[...].astype(f32), gain_ref[3:4, :], bias_ref[3:4, :]).astype(
            bf16
        )
        flip = (
            lax.broadcasted_iota(jnp.int32, (BUCKETS, BUCKETS), 0)
            + lax.broadcasted_iota(jnp.int32, (BUCKETS, BUCKETS), 1)
            == BUCKETS - 1
        ).astype(f32).astype(bf16)
        flipped = jnp.dot(flip, relative, preferred_element_type=f32).astype(bf16)
        pos_lhs[0:WIDTH, :] = (
            jnp.dot(flipped, w_ref[:, 0:WIDTH], preferred_element_type=f32).astype(bf16).T
        )
        pos_key[...] = jnp.dot(
            relative, w_ref[:, WIDTH : 2 * WIDTH], preferred_element_type=f32
        ).astype(bf16)
        projected = (
            jnp.dot(hidden_ref[...], w_ref[...], preferred_element_type=f32)
            .astype(bf16)
            .astype(f32)
        )
        for one in range(GROUP):
            proj[one] = projected[one * NEW : (one + 1) * NEW, :]

    length = lengths_ref[r]
    start = starts_ref[r]
    first = place_ref[0] * PIECE
    live = (first < length) & ((first < SINKS) | (first + PIECE > start))

    @pl.when(jnp.logical_not(live))
    def _():
        parts = lax.broadcasted_iota(jnp.int32, (2, MSG, LANES), 1)
        lanes = lax.broadcasted_iota(jnp.int32, (2, MSG, LANES), 2)
        msg_ref[...] = jnp.where(
            (parts >= 2 * CHUNKS) & ((lanes & 16) == 0), masked_score, 0.0
        )

    @pl.when(live)
    def _():
        keys = keys_ref[...]
        keys_t[...] = keys.T.astype(f32)
        q4 = proj[r, :, 0:WIDTH]
        q_all = jnp.broadcast_to(q4[:, None, :], (NEW, HEADS, WIDTH))
        row = lax.broadcasted_iota(jnp.int32, (NEW, HEADS, WIDTH), 1)
        col_head = lax.broadcasted_iota(jnp.int32, (NEW, HEADS, WIDTH), 2) >> 6
        row_head = 2 * (row & (CHUNKS - 1)) + (row >> 3)
        own_head = row_head == col_head
        queries = (
            jnp.where(own_head, q_all, 0.0).reshape(table_rows, WIDTH).astype(bf16)
        )
        content = dot_nt(queries, keys)
        to_table = dot_nt(queries, pos_key[...])
        high = to_table.astype(bf16)
        rest = to_table - high.astype(f32)
        mid = rest.astype(bf16)
        low = (rest - mid.astype(f32)).astype(bf16)
        to_pos = []
        for t in range(NEW):
            span = slice(t * HEADS, (t + 1) * HEADS)
            for part, piece in enumerate((high, mid, low)):
                pos_lhs[WIDTH + part * HEADS : WIDTH + (part + 1) * HEADS, :] = piece[span, :]
            halves = []
            for half in range(PIECE // TILE):
                cols = slice(half * TILE, (half + 1) * TILE)
                chosen = (
                    lax.broadcasted_iota(jnp.int32, (BUCKETS, TILE), 0)
                    == buckets_ref[t : t + 1, cols]
                ).astype(f32).astype(bf16)
                picked = jnp.dot(pos_lhs[...], chosen, preferred_element_type=f32)
                product = picked[0:WIDTH] * keys_t[:, cols]
                heads_sum = jnp.sum(product.reshape(HEADS, HEAD_DIM, TILE), axis=1)
                for sub in range(TILE // LANES):
                    at = (half * (TILE // LANES) + sub) * table_rows + t * HEADS
                    from_pos[at : at + HEADS, :] = heads_sum[:, sub * LANES : (sub + 1) * LANES]
                halves.append(
                    picked[WIDTH : WIDTH + HEADS]
                    + picked[WIDTH + HEADS : WIDTH + 2 * HEADS]
                    + picked[WIDTH + 2 * HEADS : WIDTH + 3 * HEADS]
                )
            to_pos.append(jnp.concatenate(halves, axis=1))
        from_parts = []
        for t in range(NEW):
            for j in range(2):
                from_parts.append(
                    jnp.concatenate(
                        [
                            from_pos[pl.ds(sub * table_rows + t * HEADS + j, CHUNKS, stride=2), :]
                            for sub in range(PIECE // LANES)
                        ],
                        axis=1,
                    )
                )
        total = content + jnp.concatenate(to_pos, axis=0) + jnp.concatenate(from_parts, axis=0)
        position = first + lax.broadcasted_iota(jnp.int32, (table_rows, PIECE), 1)
        allowed = (position < length) & ((position < SINKS) | (position >= start))
        scores = jnp.where(allowed, total * score_scale, masked_score)
        top = jnp.max(scores, axis=1, keepdims=True)
        weights = jnp.where(allowed, jnp.exp(scores - top), 0.0)
        sums = jnp.sum(weights, axis=1, keepdims=True)
        wide = jnp.dot(weights.astype(bf16), values_ref[...], preferred_element_type=f32)
        numer = jnp.sum(
            jnp.where(own_head, wide.reshape(NEW, HEADS, WIDTH), 0.0), axis=1
        )
        rows_to_tiles(numer, stage, NEW)
        for pair in range(2):
            msg_ref[pair, 0 : 2 * CHUNKS, :] = stage[
                pair * 2 * CHUNKS : (pair + 1) * 2 * CHUNKS, :
            ]
            columns = []
            for token in (2 * pair, 2 * pair + 1):
                for j in range(2):
                    at = token * HEADS + j * CHUNKS
                    columns.append(top[at : at + CHUNKS])
                    columns.append(sums[at : at + CHUNKS])
            msg_ref[pair, 2 * CHUNKS : MSG, :] = pack_ml(columns, lane)

    @pl.when(r == place_ref[0] // 2)
    def _():
        odd = lax.rem(place_ref[0], 2)
        q4 = proj[r, :, 0:WIDTH]
        k4 = proj[r, :, WIDTH : 2 * WIDTH]
        v4 = proj[r, :, 2 * WIDTH : 3 * WIDTH]
        wanted = new_ref[...]
        picked = (
            lax.broadcasted_iota(jnp.int32, (NEW * NEW, BUCKETS), 1) == wanted
        ).astype(f32).astype(bf16)
        pq = dot_nt(picked, pos_lhs[0:WIDTH, :])
        pk = jnp.dot(picked, pos_key[...], preferred_element_type=f32)
        q16 = jnp.broadcast_to(q4[:, None, :], (NEW, NEW, WIDTH)).reshape(NEW * NEW, WIDTH)
        k16 = jnp.broadcast_to(k4[None], (NEW, NEW, WIDTH)).reshape(NEW * NEW, WIDTH)
        rows_to_tiles(q16 * (k16 + pk) + k16 * pq, fresh_stage, NEW * NEW)
        rows_to_tiles(v4, stage, NEW)
        columns = []
        for i in range(2):
            token = 2 * odd + i
            spread = []
            for u in range(NEW):
                at = pl.multiple_of((token * NEW + u) * CHUNKS, CHUNKS)
                terms = fresh_stage[pl.ds(at, CHUNKS), :]
                even = jnp.sum(jnp.where(lane < HEAD_DIM, terms, 0.0), axis=1, keepdims=True)
                other = jnp.sum(jnp.where(lane >= HEAD_DIM, terms, 0.0), axis=1, keepdims=True)
                spread.append(
                    jnp.where(u <= token, spread_pair(even, other, lane) * score_scale, masked_score)
                )
            top = functools.reduce(jnp.maximum, spread)
            sums = jnp.zeros_like(top)
            numer = jnp.zeros_like(top)
            for u in range(NEW):
                weight = jnp.where(u <= token, jnp.exp(spread[u] - top), 0.0)
                sums = sums + weight
                numer = numer + weight.astype(bf16).astype(f32) * stage[
                    u * CHUNKS : (u + 1) * CHUNKS, :
                ]
            fresh_ref[i * CHUNKS : (i + 1) * CHUNKS, :] = numer
            for at in (0, HEAD_DIM):
                columns.append(top[:, at : at + 1])
                columns.append(sums[:, at : at + 1])
        fresh_ref[2 * CHUNKS : MSG, :] = pack_ml(columns, lane)


def attend_call(
    lengths, starts, place, hidden, rel, gains, biases, w_qkv, keys, values, buckets, new_buckets
):
    def whole(shape):
        return pl.BlockSpec(shape, lambda r, *_: (0,) * len(shape), pipeline_mode=pl.Buffered(1))

    return pl.pallas_call(
        attend_kernel,
        out_shape=(
            jax.ShapeDtypeStruct((SEQ_N, MSG, LANES), f32),
            jax.ShapeDtypeStruct((MSG, LANES), f32),
        ),
        grid_spec=pltpu.PrefetchScalarGridSpec(
            num_scalar_prefetch=3,
            grid=(GROUP,),
            in_specs=[
                whole((ROWS, WIDTH)),
                whole((BUCKETS, WIDTH)),
                whole((4, WIDTH)),
                whole((4, WIDTH)),
                whole((WIDTH, 3 * WIDTH)),
                pl.BlockSpec((None, PIECE, WIDTH), lambda r, *_: (r, 0, 0)),
                pl.BlockSpec((None, PIECE, WIDTH), lambda r, *_: (r, 0, 0)),
                pl.BlockSpec((None, NEW, PIECE), lambda r, *_: (r, 0, 0)),
                pl.BlockSpec((None, NEW * NEW, 1), lambda r, *_: (r, 0, 0)),
            ],
            out_specs=(
                pl.BlockSpec((2, MSG, LANES), lambda r, *_: (r, 0, 0)),
                pl.BlockSpec((MSG, LANES), lambda r, *_: (0, 0)),
            ),
            scratch_shapes=[
                pltpu.VMEM((GROUP, NEW, 3 * WIDTH), f32),
                pltpu.VMEM((WIDTH + 3 * HEADS, BUCKETS), bf16),
                pltpu.VMEM((BUCKETS, WIDTH), bf16),
                pltpu.VMEM((WIDTH, PIECE), f32),
                pltpu.VMEM((PIECE // LANES * NEW * HEADS, LANES), f32),
                pltpu.VMEM((NEW * CHUNKS, LANES), f32),
                pltpu.VMEM((NEW * NEW * CHUNKS, LANES), f32),
            ],
        ),
        compiler_params=pltpu.CompilerParams(vmem_limit_bytes=56 << 20),
        name="attend_piece",
    )(lengths, starts, place, hidden, rel, gains, biases, w_qkv, keys, values, buckets, new_buckets)


def finish_kernel(
    msg_ref, fresh_ref, hidden_ref, gain_ref, bias_ref, w_out_ref, w_in_ref, w_down_ref,
    out_ref, land, tiles, got, stage, rows_f,
    a_send, a_recv, b_send, b_recv, c_send, c_recv, d_send, d_recv,
):
    me = lax.axis_index("seq")
    barrier = pltpu.get_barrier_semaphore()
    for k in range(1, SEQ_N):
        pl.semaphore_signal(
            barrier, inc=1, device_id={"seq": lax.rem(me + k, SEQ_N)}, device_id_type=MESH
        )
    pl.semaphore_wait(barrier, SEQ_N - 1)
    lane = lax.broadcasted_iota(jnp.int32, (CHUNKS, LANES), 1)
    copies = seq_scatter(me, msg_ref, land, a_send, a_recv)
    land[0] = msg_ref[me]
    wait_all(copies)
    sources = [land.at[k] for k in range(SEQ_N)] + [fresh_ref]
    for i in range(2):
        tops, sums = [], []
        for source in sources:
            ml = source[2 * CHUNKS : MSG, :]
            at = i * HEAD_DIM
            tops.append(spread_pair(ml[:, at : at + 1], ml[:, at + 32 : at + 33], lane))
            sums.append(spread_pair(ml[:, at + 16 : at + 17], ml[:, at + 48 : at + 49], lane))
        top = functools.reduce(jnp.maximum, tops)
        numer = jnp.zeros_like(top)
        denom = jnp.zeros_like(top)
        for source, one, part in zip(sources, tops, sums):
            factor = jnp.exp(one - top)
            numer = numer + factor * source[i * CHUNKS : (i + 1) * CHUNKS, :]
            denom = denom + factor * part
        rows_f[i * CHUNKS : (i + 1) * CHUNKS, :] = numer / denom
    attended = tiles_to_rows(rows_f, 2).astype(bf16)
    rows_f[...] = hidden_ref[me].astype(f32)
    hidden_zero = tiles_to_rows(rows_f, 2)
    attn_out = jnp.dot(attended, w_out_ref[...], preferred_element_type=f32)
    hidden_one = (
        layer_norm(hidden_zero + attn_out, gain_ref[1:2, :], bias_ref[1:2, :])
        .astype(bf16)
        .astype(f32)
    )
    rows_to_tiles(hidden_one, rows_f, 2)
    tiles[0, me] = rows_f[...].astype(bf16)
    wait_all(seq_gather(me, tiles.at[0], b_send, b_recv))
    stage[...] = tiles[0].astype(f32).reshape(ROWS * CHUNKS, LANES)
    everyone = tiles_to_rows(stage, ROWS).astype(bf16)
    inner = dot_nt(everyone, w_in_ref[...])
    inner = (0.5 * inner * (1.0 + lax.erf(inner * math.sqrt(0.5)))).astype(bf16)
    rows_to_tiles(jnp.dot(inner, w_down_ref[...], preferred_element_type=f32), stage, ROWS)
    tiles[1] = stage[...].reshape(SEQ_N, 2 * CHUNKS, LANES).astype(bf16)
    copies = seq_scatter(me, tiles.at[1], got, c_send, c_recv)
    total = tiles[1, me].astype(f32)
    for k in range(1, SEQ_N):
        copies[k - 1].wait()
        total = total + got[k].astype(f32)
    rows_f[...] = total
    mlp_out = tiles_to_rows(rows_f, 2)
    layer_out = layer_norm(hidden_one + mlp_out, gain_ref[2:3, :], bias_ref[2:3, :])
    rows_to_tiles(layer_out, rows_f, 2)
    tiles[2, me] = rows_f[...].astype(bf16)
    wait_all(seq_gather(me, tiles.at[2], d_send, d_recv))
    stage[...] = tiles[2].astype(f32).reshape(ROWS * CHUNKS, LANES)
    out_ref[...] = tiles_to_rows(stage, ROWS).astype(bf16)


def finish_call(msg, fresh, hidden, gains, biases, w_out, w_in, w_down):
    slot = (SEQ_N, 2 * CHUNKS, LANES)
    return pl.pallas_call(
        finish_kernel,
        out_shape=jax.ShapeDtypeStruct((ROWS, WIDTH), bf16),
        in_specs=[pl.BlockSpec(memory_space=pltpu.VMEM)] * 8,
        out_specs=pl.BlockSpec(memory_space=pltpu.VMEM),
        scratch_shapes=[
            pltpu.VMEM((SEQ_N, MSG, LANES), f32),
            pltpu.VMEM((3,) + slot, bf16),
            pltpu.VMEM(slot, bf16),
            pltpu.VMEM((ROWS * CHUNKS, LANES), f32),
            pltpu.VMEM((2 * CHUNKS, LANES), f32),
        ]
        + [pltpu.SemaphoreType.DMA((SEQ_N,))] * 8,
        compiler_params=pltpu.CompilerParams(
            collective_id=1, has_side_effects=True, vmem_limit_bytes=32 << 20
        ),
        name="finish_layer",
    )(msg, fresh, hidden, gains, biases, w_out, w_in, w_down)


def shards(
    token_ids,
    embed_table,
    ln_gains,
    ln_biases,
    rel_table,
    w_qkv,
    w_out,
    cache_keys,
    cache_values,
    lengths,
    window_starts,
    cache_buckets,
    new_buckets,
    w_in,
    w_down,
):
    place = lax.axis_index("seq").astype(jnp.int32).reshape(1)
    hidden_zero = embed_call(token_ids.reshape(-1, 1), embed_table, ln_gains, ln_biases)
    messages, fresh = attend_call(
        lengths, window_starts, place, hidden_zero, rel_table, ln_gains, ln_biases, w_qkv,
        cache_keys, cache_values, cache_buckets, new_buckets.reshape(GROUP, NEW * NEW, 1),
    )
    hidden_tiles = hidden_zero.reshape(SEQ_N, 2 * CHUNKS, LANES)
    layer_out = finish_call(
        messages, fresh, hidden_tiles, ln_gains, ln_biases, w_out, w_in, w_down
    )
    return layer_out.reshape(GROUP, NEW, WIDTH)


def solution(mesh):
    in_specs = (
        P(),
        P(("req", "seq"), None),
        P(),
        P(),
        P(),
        P(),
        P(),
        P("req", "seq", None),
        P("req", "seq", None),
        P("req"),
        P("req"),
        P("req", None, "seq"),
        P("req", None, None),
        P("seq", None),
        P("seq", None),
    )
    out_specs = P("req", None, None)
    return jax.shard_map(shards, mesh=mesh, in_specs=in_specs, out_specs=out_specs, check_vma=False)
```

time: 753 us -> 98.8 us (0.13)
  matrix products: 244 us -> 0 us
  waiting for transfers between devices: 190 us -> 0 us
  blocking collectives: 143 us -> 0 us
  local copies, waits for them, and re-layouts: 115 us -> 8.31 us
  Pallas kernels: 0 us -> 89.9 us
  other arithmetic: 44.1 us -> 0 us
  between operations: 13.6 us -> 0.13 us
    dot_general x50 -> x0, matrix products: 244 us -> none  [the longest x8 137 us: piece_scores(): jnp.einsum('tpb,hpb->htp', selector, key_table, precision=lax.Precision.H...]
    psum x3 -> x0, waiting for transfers between devices: 190 us -> none  [the longest x1 101 us: shards(): summed = lax.psum(looked_up, ('req', 'seq'))]
    pallas_call x0 -> x3, Pallas kernels: none -> 89.9 us  [the longest x1 39.3 us: attend_call(): pl.pallas_call(attend_kernel, out_shape=(jax.ShapeDtypeStruct((SEQ_N, MSG...]
    pmax x1 -> x0, blocking collectives: 73.2 us -> none  [shards(): lax.pmax(jnp.max(scores, axis=-1), 'seq')]
    psum x1 -> x0, blocking collectives: 69.6 us -> none  [shards(): numer_total, denom_total = lax.psum((numerators, denominators), 'seq')]
    dynamic_slice x40 -> x0, local copies, waits for them, and re-layouts: 33.2 us -> none  [shards(): lax.map(score_step, (queries, query_table, key_heads, cache_buckets, leng...]
    gather x7 -> x0, local copies, waits for them, and re-layouts: 22.4 us -> none  [the longest x5 21.2 us: shards(): jnp.take_along_axis(query_table, jnp.broadcast_to(new_buckets[:, None], (...]
    unnamed x49 -> x25, local copies, waits for them, and re-layouts: 24.5 us -> 6.05 us
  transfers between devices with their start and end apart: 3 -> 0, of which waited for: 3 -> 0; matrix products, arithmetic and copies ran while one was open for 7% -> 0% of each run, Pallas kernels for 0% -> 0%
where the time goes in v1:
time: 98.8 us; the launch traced here: 98.4 us
  Pallas kernels  89.9 us (91%)
  local copies, waits for them, and re-layouts  8.31 us (8%)
    pallas_call x1, Pallas kernels, attend_call(): pl.pallas_call(attend_kernel, out_shape=(jax.ShapeDtypeStruct((SEQ_N, MSG...  39.3 us
    pallas_call x1, Pallas kernels, embed_call(): pl.pallas_call(embed_kernel, out_shape=jax.ShapeDtypeStruct((ROWS, WIDTH)...  25.9 us
    pallas_call x1, Pallas kernels, finish_call(): pl.pallas_call(finish_kernel, out_shape=jax.ShapeDtypeStruct((ROWS, WIDTH...  24.7 us
    unnamed x25, local copies, waits for them, and re-layouts  6.05 us

profile of v1, /device:TPU:0, one launch (start us, length us, event | category | flops | bytes accessed | tf_op | source)
XLA Modules:
  0.0 98.4 jit_solution(10320932293439287321)
XLA Ops:
  0.0 0.8 copy.18
  0.8 0.1 reshape.20.ids_ref
  0.9 0.0 copy-start.1
  0.9 1.6 %copy-done.1 = bf16[1000,1024]{1,0:T(8,128)(2,1)S(1)} copy-done((bf16[1000,1024]{1,0:T(8,128)(2,1)S(1)}, bf16[1000,1024]{1,0:T(8,128)(2,1)}, u32[]{:S(2)}) %copy-start.1) | copy-done | bytes 2048024
  2.4 0.0 copy-start.7
  2.4 0.7 copy-done.7
  3.2 0.0 copy-start.9
  3.2 0.7 copy-done.9
  3.9 25.9 %embed_exchange.1.hidden_ref = bf16[32,1024]{1,0:T(8,128)(2,1)S(1)} custom-call(s32[256,1]{1,0:T(8,128)S(1)} %reshape.20.ids_ref, bf16[1000,1024]{1,0:T(8,128)(2,1)S(1)} %copy-done.1, f32[4,1024]{1,0:T(4,128)S(1)} %copy-done.7, f32[4,1024]{1,0:T(4,128)S(1)} %copy-done.9), custom_call_target="tpu_custom_call" | custom-call | tf_op jit(solution)/shard_map/embed_exchange/pallas_call | solution.py:153
  29.8 0.0 copy-start.2
  29.8 0.6 copy-done.2
  30.4 1.5 %copy.20.new_ref = s32[8,16,1]{2,1,0:T(8,128)} copy(s32[8,16,1]{0,1,2:T(8,128)} %bitcast.2) | data formatting | bytes 1024 | tf_op jit(solution)/shard_map/reshape | solution.py:511
  31.9 0.0 copy-start.3
  31.9 0.0 copy-start
  31.9 0.0 copy-start.4
  31.9 0.0 copy-start.5
  31.9 0.0 copy-start.8
  31.9 0.0 copy-start.10
  31.9 39.3 %attend_piece.1 = (f32[16,24,128]{2,1,0:T(8,128)}, f32[24,128]{1,0:T(8,128)}) custom-call(s32[8]{0:T(128)} %lengths_ref.1, s32[8]{0:T(128)} %starts_ref.1, s32[1]{0:T(128)} %bitcast.place_ref, bf16[32,1024]{1,0:T(8,128)(2,1)} %copy-done.2, bf16[512,1024]{1,0:T(8,128)(2,1)} %rel_ref.1, f32[4,1024]{1,0:T(4,128)} %gain_ref.5, f32[4,1024]{1,0:T(4,128)} %bias_ref.5, ...), custom_call_target="tpu_custom_call" | custom-call | tf_op jit(solution)/shard_map/attend_piece/pallas_call | solution.py:364
  71.2 0.0 copy-done.3
  71.3 0.0 copy-done
  71.3 0.0 copy-done.4
  71.3 0.0 copy-done.5
  71.3 0.0 copy-done.8
  71.3 0.0 copy-done.10
  71.3 0.0 copy-start.6
  71.3 0.9 copy-done.6
  72.3 0.0 copy-start.11
  72.3 0.7 copy-done.11
  73.0 24.7 %finish_layer.1 = bf16[32,1024]{1,0:T(8,128)(2,1)S(1)} custom-call(f32[16,24,128]{2,1,0:T(8,128)S(1)} %copy-done.6, f32[24,128]{1,0:T(8,128)S(1)} %copy-done.11, bf16[16,16,128]{2,1,0:T(8,128)(2,1)S(1)} %reshape.18.hidden_ref, f32[4,1024]{1,0:T(4,128)S(1)} %copy-done.8, f32[4,1024]{1,0:T(4,128)S(1)} %copy-done.10, bf16[1024,1024]{1,0:T(8,128)(2,1)S(1)} %copy-done, ...), custom_call_target="tpu_custom_call" | custom-call | tf_op jit(solution)/shard_map/finish_layer/pallas_call | solution.py:470
  97.7 0.7 reshape.19
  (1 shorter events, 0.0 us)
Async XLA Ops:
  0.9 1.6 %copy-start.1 = (bf16[1000,1024]{1,0:T(8,128)(2,1)S(1)}, bf16[1000,1024]{1,0:T(8,128)(2,1)}, u32[]{:S(2)}) copy-start(bf16[1000,1024]{1,0:T(8,128)(2,1)} %table_ref.1) | copy-start | bytes 6144004
  2.4 0.7 copy-start.7
  3.2 0.7 copy-start.9
  29.8 0.6 copy-start.2
  31.9 39.3 %copy-start.3 = (bf16[32,1024]{1,0:T(8,128)(2,1)S(1)}, bf16[32,1024]{1,0:T(8,128)(2,1)}, u32[]{:S(2)}) copy-start(bf16[32,1024]{1,0:T(8,128)(2,1)} %copy-done.2) | copy-start | bytes 196612
  31.9 39.4 %copy-start = (bf16[1024,1024]{1,0:T(8,128)(2,1)S(1)}, bf16[1024,1024]{1,0:T(8,128)(2,1)}, u32[]{:S(2)}) copy-start(bf16[1024,1024]{1,0:T(8,128)(2,1)} %w_out_ref.1) | copy-start | bytes 6291460
  31.9 39.4 %copy-start.4 = (bf16[256,1024]{1,0:T(8,128)(2,1)S(1)}, bf16[256,1024]{1,0:T(8,128)(2,1)}, u32[]{:S(2)}) copy-start(bf16[256,1024]{1,0:T(8,128)(2,1)} %w_in_ref.1) | copy-start | bytes 1572868
  31.9 39.4 %copy-start.5 = (bf16[256,1024]{1,0:T(8,128)(2,1)S(1)}, bf16[256,1024]{1,0:T(8,128)(2,1)}, u32[]{:S(2)}) copy-start(bf16[256,1024]{1,0:T(8,128)(2,1)} %w_down_ref.1) | copy-start | bytes 1572868
  31.9 39.4 %copy-start.8 = (f32[4,1024]{1,0:T(4,128)S(1)}, f32[4,1024]{1,0:T(4,128)}, u32[]{:S(2)}) copy-start(f32[4,1024]{1,0:T(4,128)} %gain_ref.5) | copy-start | bytes 49156
  31.9 39.4 %copy-start.10 = (f32[4,1024]{1,0:T(4,128)S(1)}, f32[4,1024]{1,0:T(4,128)}, u32[]{:S(2)}) copy-start(f32[4,1024]{1,0:T(4,128)} %bias_ref.5) | copy-start | bytes 49156
  71.3 0.9 copy-start.6
  72.3 0.7 copy-start.11

commit v2 on v0

v2 whole, which is shorter than its diff:
```python
import functools
import math

import jax
import jax.numpy as jnp
from jax import lax
from jax.experimental import pallas as pl
from jax.experimental.pallas import tpu as pltpu
from jax.sharding import PartitionSpec as P

HEADS = 16
HEAD_DIM = 64
SINKS = 4
NEW = 4
WIDTH = 1024
REQ_N = 8
SEQ_N = 16
GROUP = 8
ROWS = GROUP * NEW
PIECE = 512
BUCKETS = 512
TILE = 256
LANES = 128
CHUNKS = WIDTH // LANES
MSG = 24
HOOKS = (2, 3, 4)

norm_epsilon = 1e-06
masked_score = -1e30
score_scale = 1.0 / math.sqrt(3 * HEAD_DIM)
MESH = pl.DeviceIdType.MESH
f32 = jnp.float32
bf16 = jnp.bfloat16


def layer_norm(values, gain, shift):
    center = values - jnp.mean(values, axis=-1, keepdims=True)
    spread = jnp.mean(center * center, axis=-1, keepdims=True)
    return center * lax.rsqrt(spread + norm_epsilon) * gain + shift


def dot_nt(a, b):
    return lax.dot_general(a, b, (((1,), (1,)), ((), ())), preferred_element_type=f32)


def rows_to_tiles(rows, stage, count):
    for c in range(CHUNKS):
        stage[pl.ds(c, count, stride=CHUNKS), :] = rows[:, c * LANES : (c + 1) * LANES]


def tiles_to_rows(stage, count):
    return jnp.concatenate(
        [stage[pl.ds(c, count, stride=CHUNKS), :] for c in range(CHUNKS)], axis=1
    )


def seq_copy(src, dst, send_sem, recv_sem, peer):
    return pltpu.make_async_remote_copy(
        src_ref=src,
        dst_ref=dst,
        send_sem=send_sem,
        recv_sem=recv_sem,
        device_id={"seq": peer},
        device_id_type=MESH,
    )


def seq_scatter(me, send, recv, send_sems, recv_sems):
    copies = []
    for k in range(1, SEQ_N):
        peer = lax.rem(me + k, SEQ_N)
        copy = seq_copy(send.at[peer], recv.at[k], send_sems.at[k], recv_sems.at[k], peer)
        copies.append(copy)
    return copies


def seq_gather(me, buf, send_sems, recv_sems):
    copies = []
    for k in range(1, SEQ_N):
        peer = lax.rem(me + k, SEQ_N)
        copy = seq_copy(buf.at[me], buf.at[me], send_sems.at[k], recv_sems.at[k], peer)
        copies.append(copy)
    return copies


def start_all(copies):
    for copy in copies:
        copy.start()


def wait_all(copies):
    for copy in copies:
        copy.wait()


def spread_pair(column_even, column_odd, lane):
    return jnp.where(lane < HEAD_DIM, column_even, column_odd)


def pack_ml(values, lane):
    out = jnp.zeros((CHUNKS, LANES), f32)
    for g, value in enumerate(values):
        out = jnp.where((lane >> 4) == g, value, out)
    return out


def layer_kernel(
    ids_ref, table_hbm, gain_ref, bias_ref, rel_hbm, w_hbm, w_out_hbm, keys_hbm, values_hbm,
    lengths_ref, starts_ref, buckets_ref, new_ref, w_in_hbm, w_down_hbm,
    out_ref,
    table, rel, w_qkv, w_out, keys, values, w_in, w_down,
    send, land, stage, tiles, got, hid, rows_f, proj, pos_lhs, pos_key, keys_t, from_pos, queries,
    q_table, msgs, inbox, fresh, fresh_stage, picks,
    local_sems, key_sems, value_sems,
    req_send, req_recv, rs_send, rs_recv, ag_send, ag_recv,
    a_send, a_recv, b_send, b_recv, c_send, c_recv, d_send, d_recv,
):
    me = lax.axis_index("seq")
    req = lax.axis_index("req")
    table_rows = NEW * HEADS
    lane = lax.broadcasted_iota(jnp.int32, (CHUNKS, LANES), 1)

    def local(src, dst, index):
        return pltpu.make_async_copy(src, dst, local_sems.at[index])

    table_copy = local(table_hbm, table, 0)
    rel_copy = local(rel_hbm, rel, 1)
    w_copy = local(w_hbm, w_qkv, 2)
    out_copy = local(w_out_hbm, w_out, 3)
    in_copy = local(w_in_hbm, w_in, 4)
    down_copy = local(w_down_hbm, w_down, 5)

    def key_copy(r):
        return pltpu.make_async_copy(keys_hbm.at[r], keys.at[r], key_sems.at[r])

    def value_copy(r):
        return pltpu.make_async_copy(values_hbm.at[r], values.at[r], value_sems.at[r])

    table_copy.start()
    rel_copy.start()
    w_copy.start()
    barrier = pltpu.get_barrier_semaphore()
    for k in range(1, SEQ_N):
        pl.semaphore_signal(
            barrier, inc=1, device_id={"seq": lax.rem(me + k, SEQ_N)}, device_id_type=MESH
        )
    for k in range(1, REQ_N):
        pl.semaphore_signal(
            barrier, inc=1, device_id={"req": lax.rem(req + k, REQ_N)}, device_id_type=MESH
        )
    for r in range(GROUP):
        key_copy(r).start()

    vocab_rows = table.shape[0]
    ids = jnp.concatenate(
        [
            ids_ref[g * GROUP : (g + 1) * GROUP, t : t + 1]
            for g in range(REQ_N)
            for t in range(NEW)
        ],
        axis=0,
    ) - (req * SEQ_N + me) * vocab_rows
    one_hot = (
        lax.broadcasted_iota(jnp.int32, (REQ_N * ROWS, vocab_rows), 1) == ids
    ).astype(f32).astype(bf16)
    table_copy.wait()
    send[...] = (
        jnp.dot(one_hot, table[...], preferred_element_type=f32)
        .astype(bf16)
        .reshape(REQ_N, ROWS, WIDTH)
    )
    pl.semaphore_wait(barrier, SEQ_N - 1 + REQ_N - 1)

    def req_copies():
        copies = []
        for k in range(1, REQ_N):
            peer = lax.rem(req + k, REQ_N)
            copies.append(
                pltpu.make_async_remote_copy(
                    src_ref=send.at[peer],
                    dst_ref=land.at[k],
                    send_sem=req_send.at[k],
                    recv_sem=req_recv.at[k],
                    device_id={"req": peer},
                    device_id_type=MESH,
                )
            )
        return copies

    for copy in req_copies():
        copy.start()
    for r in range(GROUP):
        value_copy(r).start()
    out_copy.start()
    in_copy.start()
    down_copy.start()

    rel_copy.wait()
    relative = layer_norm(rel[...].astype(f32), gain_ref[3:4, :], bias_ref[3:4, :]).astype(bf16)
    flip = (
        lax.broadcasted_iota(jnp.int32, (BUCKETS, BUCKETS), 0)
        + lax.broadcasted_iota(jnp.int32, (BUCKETS, BUCKETS), 1)
        == BUCKETS - 1
    ).astype(f32).astype(bf16)
    flipped = jnp.dot(flip, relative, preferred_element_type=f32).astype(bf16)
    w_copy.wait()
    pos_lhs[...] = (
        jnp.dot(flipped, w_qkv[:, 0:WIDTH], preferred_element_type=f32).astype(bf16).T
    )
    pos_key[...] = jnp.dot(
        relative, w_qkv[:, WIDTH : 2 * WIDTH], preferred_element_type=f32
    ).astype(bf16)

    def own_head():
        row = lax.broadcasted_iota(jnp.int32, (NEW, HEADS, WIDTH), 1)
        col_head = lax.broadcasted_iota(jnp.int32, (NEW, HEADS, WIDTH), 2) >> 6
        return 2 * (row & (CHUNKS - 1)) + (row >> 3) == col_head

    def from_pos_step(r, carry):
        @pl.when(r == HOOKS[0])
        def _():
            copies = req_copies()
            total = send[req].astype(f32)
            for k in range(1, REQ_N):
                copies[k - 1].wait()
                total = total + land[k].astype(f32)
            for t in range(NEW):
                for c in range(CHUNKS):
                    stage[pl.ds(t * CHUNKS + c, GROUP, stride=NEW * CHUNKS), :] = total[
                        t * GROUP : (t + 1) * GROUP, c * LANES : (c + 1) * LANES
                    ]
            tiles[0] = stage[...].reshape(SEQ_N, 2 * CHUNKS, LANES).astype(bf16)
            start_all(seq_scatter(me, tiles.at[0], got.at[0], rs_send, rs_recv))

        @pl.when(r == HOOKS[1])
        def _():
            copies = seq_scatter(me, tiles.at[0], got.at[0], rs_send, rs_recv)
            own = tiles[0, me].astype(f32)
            for k in range(1, SEQ_N):
                copies[k - 1].wait()
                own = own + got[0, k].astype(f32)
            rows_f[...] = own
            hidden = layer_norm(tiles_to_rows(rows_f, 2), gain_ref[0:1, :], bias_ref[0:1, :])
            rows_to_tiles(hidden, rows_f, 2)
            hid[0, me] = rows_f[...].astype(bf16)
            start_all(seq_gather(me, hid.at[0], ag_send, ag_recv))

        @pl.when(r == HOOKS[2])
        def _():
            wait_all(seq_gather(me, hid.at[0], ag_send, ag_recv))
            stage[...] = hid[0].astype(f32).reshape(ROWS * CHUNKS, LANES)
            hidden = tiles_to_rows(stage, ROWS).astype(bf16)
            projected = (
                jnp.dot(hidden, w_qkv[...], preferred_element_type=f32).astype(bf16).astype(f32)
            )
            mine = own_head()
            for one in range(GROUP):
                block = projected[one * NEW : (one + 1) * NEW, :]
                proj[one] = block
                q_all = jnp.broadcast_to(block[:, None, 0:WIDTH], (NEW, HEADS, WIDTH))
                queries[one * table_rows : (one + 1) * table_rows, :] = (
                    jnp.where(mine, q_all, 0.0).reshape(table_rows, WIDTH).astype(bf16)
                )
            q_table[...] = dot_nt(queries[...], pos_key[...])

        key_copy(r).wait()
        keys_t[...] = keys[r].T.astype(f32)
        for t in range(NEW):
            for half in range(PIECE // TILE):
                cols = slice(half * TILE, (half + 1) * TILE)
                chosen = (
                    lax.broadcasted_iota(jnp.int32, (BUCKETS, TILE), 0)
                    == buckets_ref[r, t : t + 1, cols]
                ).astype(f32).astype(bf16)
                product = (
                    jnp.dot(pos_lhs[...], chosen, preferred_element_type=f32) * keys_t[:, cols]
                )
                heads_sum = jnp.sum(product.reshape(HEADS, HEAD_DIM, TILE), axis=1)
                for sub in range(TILE // LANES):
                    at = (half * (TILE // LANES) + sub) * table_rows + t * HEADS
                    from_pos[r, at : at + HEADS, :] = heads_sum[
                        :, sub * LANES : (sub + 1) * LANES
                    ]
        return carry

    lax.fori_loop(0, GROUP, from_pos_step, 0)

    first = me * PIECE

    def message_copy(r, pair):
        peer = 2 * r + pair
        return seq_copy(
            msgs.at[peer], inbox.at[me], a_send.at[peer], a_recv.at[me], peer
        )

    def attend_step(r, carry):
        value_copy(r).wait()
        span = pl.ds(pl.multiple_of(r * table_rows, table_rows), table_rows)
        content = dot_nt(queries[span, :], keys[r])
        parts = []
        for t in range(NEW):
            tables = [
                q_table[
                    pl.ds(pl.multiple_of(r * table_rows + t * HEADS, HEADS), HEADS),
                    kb * LANES : (kb + 1) * LANES,
                ]
                for kb in range(BUCKETS // LANES)
            ]
            columns = []
            for sub in range(PIECE // LANES):
                bucket = jnp.broadcast_to(
                    buckets_ref[r, t : t + 1, sub * LANES : (sub + 1) * LANES], (HEADS, LANES)
                )
                low = bucket & (LANES - 1)
                high = bucket >> 7
                picked = jnp.take_along_axis(tables[0], low, axis=1)
                for kb in range(1, BUCKETS // LANES):
                    picked = jnp.where(
                        high == kb, jnp.take_along_axis(tables[kb], low, axis=1), picked
                    )
                back = jnp.concatenate(
                    [
                        from_pos[
                            r, pl.ds(sub * table_rows + t * HEADS + j, CHUNKS, stride=2), :
                        ]
                        for j in range(2)
                    ],
                    axis=0,
                )
                columns.append(picked + back)
            parts.append(jnp.concatenate(columns, axis=1))
        total = content + jnp.concatenate(parts, axis=0)
        position = first + lax.broadcasted_iota(jnp.int32, (table_rows, PIECE), 1)
        allowed = (position < lengths_ref[r]) & (
            (position < SINKS) | (position >= starts_ref[r])
        )
        scores = jnp.where(allowed, total * score_scale, masked_score)
        top = jnp.max(scores, axis=1, keepdims=True)
        weights = jnp.where(allowed, jnp.exp(scores - top), 0.0)
        sums = jnp.sum(weights, axis=1, keepdims=True)
        wide = jnp.dot(weights.astype(bf16), values[r], preferred_element_type=f32)
        numer = jnp.sum(jnp.where(own_head(), wide.reshape(NEW, HEADS, WIDTH), 0.0), axis=1)
        rows_to_tiles(numer, stage, NEW)
        for pair in range(2):
            peer = 2 * r + pair
            msgs[peer, 0 : 2 * CHUNKS, :] = stage[
                pair * 2 * CHUNKS : (pair + 1) * 2 * CHUNKS, :
            ]
            columns = []
            for token in (2 * pair, 2 * pair + 1):
                for j in range(2):
                    at = token * HEADS + j * CHUNKS
                    columns.append(top[at : at + CHUNKS])
                    columns.append(sums[at : at + CHUNKS])
            msgs[peer, 2 * CHUNKS : MSG, :] = pack_ml(columns, lane)

            @pl.when(peer != me)
            def _():
                message_copy(r, pair).start()

        return carry

    lax.fori_loop(0, GROUP, attend_step, 0)

    odd = lax.rem(me, 2)
    mine = proj[me // 2]
    wanted = new_ref[me // 2]
    for t in range(NEW):
        picks[t * NEW : (t + 1) * NEW, :] = wanted[:, t : t + 1]
    picked = (
        lax.broadcasted_iota(jnp.int32, (NEW * NEW, BUCKETS), 1) == picks[...]
    ).astype(f32).astype(bf16)
    pq = dot_nt(picked, pos_lhs[...])
    pk = jnp.dot(picked, pos_key[...], preferred_element_type=f32)
    q4, k4, v4 = (mine[:, i * WIDTH : (i + 1) * WIDTH] for i in range(3))
    q16 = jnp.broadcast_to(q4[None], (NEW, NEW, WIDTH)).reshape(NEW * NEW, WIDTH)
    k16 = jnp.broadcast_to(k4[:, None, :], (NEW, NEW, WIDTH)).reshape(NEW * NEW, WIDTH)
    rows_to_tiles(q16 * (k16 + pk) + k16 * pq, fresh_stage, NEW * NEW)
    rows_to_tiles(v4, stage, NEW)
    columns = []
    for i in range(2):
        token = 2 * odd + i
        spread = []
        for u in range(NEW):
            at = pl.multiple_of((u * NEW + token) * CHUNKS, CHUNKS)
            terms = fresh_stage[pl.ds(at, CHUNKS), :]
            even = jnp.sum(jnp.where(lane < HEAD_DIM, terms, 0.0), axis=1, keepdims=True)
            other = jnp.sum(jnp.where(lane >= HEAD_DIM, terms, 0.0), axis=1, keepdims=True)
            spread.append(
                jnp.where(u <= token, spread_pair(even, other, lane) * score_scale, masked_score)
            )
        top = functools.reduce(jnp.maximum, spread)
        sums = jnp.zeros_like(top)
        numer = jnp.zeros_like(top)
        for u in range(NEW):
            weight = jnp.where(u <= token, jnp.exp(spread[u] - top), 0.0)
            sums = sums + weight
            numer = numer + weight.astype(bf16).astype(f32) * stage[
                u * CHUNKS : (u + 1) * CHUNKS, :
            ]
        fresh[i * CHUNKS : (i + 1) * CHUNKS, :] = numer
        for at in (0, HEAD_DIM):
            columns.append(top[:, at : at + 1])
            columns.append(sums[:, at : at + 1])
    fresh[2 * CHUNKS : MSG, :] = pack_ml(columns, lane)

    inbox[me] = msgs[me]
    for k in range(1, SEQ_N):
        peer = lax.rem(me + k, SEQ_N)
        seq_copy(
            msgs.at[peer], inbox.at[peer], a_send.at[peer], a_recv.at[peer], peer
        ).wait()
    sources = [inbox.at[k] for k in range(SEQ_N)] + [fresh]
    for i in range(2):
        tops, sums = [], []
        for source in sources:
            ml = source[2 * CHUNKS : MSG, :]
            at = i * HEAD_DIM
            tops.append(spread_pair(ml[:, at : at + 1], ml[:, at + 32 : at + 33], lane))
            sums.append(spread_pair(ml[:, at + 16 : at + 17], ml[:, at + 48 : at + 49], lane))
        top = functools.reduce(jnp.maximum, tops)
        numer = jnp.zeros_like(top)
        denom = jnp.zeros_like(top)
        for source, one, part in zip(sources, tops, sums):
            factor = jnp.exp(one - top)
            numer = numer + factor * source[i * CHUNKS : (i + 1) * CHUNKS, :]
            denom = denom + factor * part
        rows_f[i * CHUNKS : (i + 1) * CHUNKS, :] = numer / denom
    attended = tiles_to_rows(rows_f, 2).astype(bf16)
    rows_f[...] = hid[0, me].astype(f32)
    hidden_zero = tiles_to_rows(rows_f, 2)
    out_copy.wait()
    attn_out = jnp.dot(attended, w_out[...], preferred_element_type=f32)
    hidden_one = (
        layer_norm(hidden_zero + attn_out, gain_ref[1:2, :], bias_ref[1:2, :])
        .astype(bf16)
        .astype(f32)
    )
    rows_to_tiles(hidden_one, rows_f, 2)
    hid[1, me] = rows_f[...].astype(bf16)
    copies = seq_gather(me, hid.at[1], b_send, b_recv)
    start_all(copies)
    in_copy.wait()
    down_copy.wait()
    wait_all(copies)
    stage[...] = hid[1].astype(f32).reshape(ROWS * CHUNKS, LANES)
    everyone = tiles_to_rows(stage, ROWS).astype(bf16)
    inner = dot_nt(everyone, w_in[...])
    inner = (0.5 * inner * (1.0 + lax.erf(inner * math.sqrt(0.5)))).astype(bf16)
    rows_to_tiles(jnp.dot(inner, w_down[...], preferred_element_type=f32), stage, ROWS)
    tiles[1] = stage[...].reshape(SEQ_N, 2 * CHUNKS, LANES).astype(bf16)
    copies = seq_scatter(me, tiles.at[1], got.at[1], c_send, c_recv)
    start_all(copies)
    total = tiles[1, me].astype(f32)
    for k in range(1, SEQ_N):
        copies[k - 1].wait()
        total = total + got[1, k].astype(f32)
    rows_f[...] = total
    mlp_out = tiles_to_rows(rows_f, 2)
    layer_out = layer_norm(hidden_one + mlp_out, gain_ref[2:3, :], bias_ref[2:3, :])
    rows_to_tiles(layer_out, rows_f, 2)
    hid[2, me] = rows_f[...].astype(bf16)
    copies = seq_gather(me, hid.at[2], d_send, d_recv)
    start_all(copies)
    wait_all(copies)
    stage[...] = hid[2].astype(f32).reshape(ROWS * CHUNKS, LANES)
    everyone = tiles_to_rows(stage, ROWS)
    for r in range(GROUP):
        out_ref[r] = everyone[r * NEW : (r + 1) * NEW, :].astype(bf16)


def shards(
    token_ids,
    embed_table,
    ln_gains,
    ln_biases,
    rel_table,
    w_qkv,
    w_out,
    cache_keys,
    cache_values,
    lengths,
    window_starts,
    cache_buckets,
    new_buckets,
    w_in,
    w_down,
):
    slot = (SEQ_N, 2 * CHUNKS, LANES)
    in_vmem = pl.BlockSpec(memory_space=pltpu.VMEM)
    in_smem = pl.BlockSpec(memory_space=pltpu.SMEM)
    in_place = pl.BlockSpec(memory_space=pl.ANY)
    return pl.pallas_call(
        layer_kernel,
        out_shape=jax.ShapeDtypeStruct((GROUP, NEW, WIDTH), bf16),
        in_specs=[
            in_vmem, in_place, in_vmem, in_vmem, in_place, in_place, in_place, in_place, in_place,
            in_smem, in_smem, in_vmem, in_vmem, in_place, in_place,
        ],
        out_specs=in_vmem,
        scratch_shapes=[
            pltpu.VMEM(embed_table.shape, bf16),
            pltpu.VMEM(rel_table.shape, bf16),
            pltpu.VMEM(w_qkv.shape, bf16),
            pltpu.VMEM(w_out.shape, bf16),
            pltpu.VMEM(cache_keys.shape, bf16),
            pltpu.VMEM(cache_values.shape, bf16),
            pltpu.VMEM(w_in.shape, bf16),
            pltpu.VMEM(w_down.shape, bf16),
            pltpu.VMEM((REQ_N, ROWS, WIDTH), bf16),
            pltpu.VMEM((REQ_N, ROWS, WIDTH), bf16),
            pltpu.VMEM((ROWS * CHUNKS, LANES), f32),
            pltpu.VMEM((2,) + slot, bf16),
            pltpu.VMEM((2,) + slot, bf16),
            pltpu.VMEM((3,) + slot, bf16),
            pltpu.VMEM((2 * CHUNKS, LANES), f32),
            pltpu.VMEM((GROUP, NEW, 3 * WIDTH), f32),
            pltpu.VMEM((WIDTH, BUCKETS), bf16),
            pltpu.VMEM((BUCKETS, WIDTH), bf16),
            pltpu.VMEM((WIDTH, PIECE), f32),
            pltpu.VMEM((GROUP, PIECE // LANES * NEW * HEADS, LANES), f32),
            pltpu.VMEM((GROUP * NEW * HEADS, WIDTH), bf16),
            pltpu.VMEM((GROUP * NEW * HEADS, BUCKETS), f32),
            pltpu.VMEM((SEQ_N, MSG, LANES), f32),
            pltpu.VMEM((SEQ_N, MSG, LANES), f32),
            pltpu.VMEM((MSG, LANES), f32),
            pltpu.VMEM((NEW * NEW * CHUNKS, LANES), f32),
            pltpu.VMEM((NEW * NEW, 1), jnp.int32),
            pltpu.SemaphoreType.DMA((6,)),
            pltpu.SemaphoreType.DMA((GROUP,)),
            pltpu.SemaphoreType.DMA((GROUP,)),
        ]
        + [pltpu.SemaphoreType.DMA((REQ_N,))] * 2
        + [pltpu.SemaphoreType.DMA((SEQ_N,))] * 12,
        compiler_params=pltpu.CompilerParams(
            collective_id=0, has_side_effects=True, vmem_limit_bytes=60 << 20
        ),
        name="decode_layer",
    )(
        token_ids, embed_table, ln_gains, ln_biases, rel_table, w_qkv, w_out, cache_keys,
        cache_values, lengths, window_starts, cache_buckets, new_buckets, w_in, w_down,
    )


def solution(mesh):
    in_specs = (
        P(),
        P(("req", "seq"), None),
        P(),
        P(),
        P(),
        P(),
        P(),
        P("req", "seq", None),
        P("req", "seq", None),
        P("req"),
        P("req"),
        P("req", None, "seq"),
        P("req", None, None),
        P("seq", None),
        P("seq", None),
    )
    out_specs = P("req", None, None)
    return jax.shard_map(shards, mesh=mesh, in_specs=in_specs, out_specs=out_specs, check_vma=False)
```

time: 753 us -> 72.6 us (0.10)
  matrix products: 244 us -> 0 us
  waiting for transfers between devices: 190 us -> 0 us
  blocking collectives: 143 us -> 0 us
  local copies, waits for them, and re-layouts: 115 us -> 4.26 us
  Pallas kernels: 0 us -> 68 us
  other arithmetic: 44.1 us -> 0 us
  between operations: 13.6 us -> 0.01 us
    dot_general x50 -> x0, matrix products: 244 us -> none  [the longest x8 137 us: piece_scores(): jnp.einsum('tpb,hpb->htp', selector, key_table, precision=lax.Precision.H...]
    psum x3 -> x0, waiting for transfers between devices: 190 us -> none  [the longest x1 101 us: shards(): summed = lax.psum(looked_up, ('req', 'seq'))]
    pmax x1 -> x0, blocking collectives: 73.2 us -> none  [shards(): lax.pmax(jnp.max(scores, axis=-1), 'seq')]
    psum x1 -> x0, blocking collectives: 69.6 us -> none  [shards(): numer_total, denom_total = lax.psum((numerators, denominators), 'seq')]
    pallas_call x0 -> x1, Pallas kernels: none -> 68 us  [shards(): pl.pallas_call(layer_kernel, out_shape=jax.ShapeDtypeStruct((GROUP, NEW,...]
    dynamic_slice x40 -> x0, local copies, waits for them, and re-layouts: 33.2 us -> none  [shards(): lax.map(score_step, (queries, query_table, key_heads, cache_buckets, leng...]
    gather x7 -> x0, local copies, waits for them, and re-layouts: 22.4 us -> none  [the longest x5 21.2 us: shards(): jnp.take_along_axis(query_table, jnp.broadcast_to(new_buckets[:, None], (...]
    unnamed x49 -> x3, local copies, waits for them, and re-layouts: 24.5 us -> 4.26 us
  transfers between devices with their start and end apart: 3 -> 0, of which waited for: 3 -> 0; matrix products, arithmetic and copies ran while one was open for 7% -> 0% of each run, Pallas kernels for 0% -> 0%
where the time goes in v2:
time: 72.6 us; the launch traced here: 72.3 us
  Pallas kernels  68 us (94%)
  local copies, waits for them, and re-layouts  4.26 us (6%)
    pallas_call x1, Pallas kernels, shards(): pl.pallas_call(layer_kernel, out_shape=jax.ShapeDtypeStruct((GROUP, NEW,...  68 us
    unnamed x3, local copies, waits for them, and re-layouts  4.26 us

profile of v2, /device:TPU:0, one launch (start us, length us, event | category | flops | bytes accessed | tf_op | source)
XLA Modules:
  0.0 72.3 jit_solution(16504686554033529353)
XLA Ops:
  0.0 1.4 %copy.17.new_ref = s32[8,4,4]{2,1,0:T(4,128)} copy(s32[8,4,4]{0,2,1:T(4,128)} %param.27) | data formatting | bytes 1024 | tf_op args[12]
  1.4 1.4 %copy.16.ids_ref = s32[64,4]{1,0:T(8,128)} copy(s32[64,4]{0,1:T(4,128)} %param.15) | data formatting | bytes 2048 | tf_op args[0]
  2.8 68.0 %decode_layer.1 = bf16[8,4,1024]{2,1,0:T(4,128)(2,1)} custom-call(s32[64,4]{1,0:T(8,128)} %copy.16.ids_ref, bf16[1000,1024]{1,0:T(8,128)(2,1)} %table_hbm.1, f32[4,1024]{1,0:T(4,128)} %gain_ref.1, f32[4,1024]{1,0:T(4,128)} %bias_ref.1, bf16[512,1024]{1,0:T(8,128)(2,1)} %rel_hbm.1, bf16[1024,3072]{1,0:T(8,128)(2,1)} %w_hbm.1, bf16[1024,1024]{1,0:T(8,128)(2,1)} %w_out_hbm.1, ...), custom_call_target="tpu_custom_call" | custom-call | tf_op jit(solution)/shard_map/decode_layer/pallas_call | solution.py:493
  70.8 1.5 %copy.19 = bf16[8,4,1024]{2,1,0:T(4,128)(2,1)} copy(bf16[8,4,1024]{2,1,0:T(4,128)(2,1)} %decode_layer.1) | data formatting | bytes 131072

commit v3 on v2

--- a/solution.py
+++ b/solution.py
@@ -22,8 +22,9 @@
 TILE = 256
 LANES = 128
 CHUNKS = WIDTH // LANES
-MSG = 24
-HOOKS = (2, 3, 4)
+SIDE = 4
+HOOKS = (3, 5, 7)
+FORWARD = 4
 
 norm_epsilon = 1e-06
 masked_score = -1e30
@@ -100,7 +101,7 @@
 def pack_ml(values, lane):
     out = jnp.zeros((CHUNKS, LANES), f32)
     for g, value in enumerate(values):
-        out = jnp.where((lane >> 4) == g, value, out)
+        out = jnp.where((lane >> 3) == g, value, out)
     return out
 
 
@@ -108,15 +109,18 @@
     ids_ref, table_hbm, gain_ref, bias_ref, rel_hbm, w_hbm, w_out_hbm, keys_hbm, values_hbm,
     lengths_ref, starts_ref, buckets_ref, new_ref, w_in_hbm, w_down_hbm,
     out_ref,
-    table, rel, w_qkv, w_out, keys, values, w_in, w_down,
-    send, land, stage, tiles, got, hid, rows_f, proj, pos_lhs, pos_key, keys_t, from_pos, queries,
-    q_table, msgs, inbox, fresh, fresh_stage, picks,
+    table, rel, w_qkv, w_out, keys, values, w_ff, ids_pad,
+    send, land, stage, tiles, got, hid, h_zero, rows_f, att, proj, pos_lhs, pos_key, keys_t,
+    from_pos, queries, q_table, msg_numer, msg_ml, in_numer, in_ml, fresh_numer, fresh_ml,
+    fresh_stage, v_stage, picks, partial, final,
     local_sems, key_sems, value_sems,
     req_send, req_recv, rs_send, rs_recv, ag_send, ag_recv,
-    a_send, a_recv, b_send, b_recv, c_send, c_recv, d_send, d_recv,
+    n_send, n_recv, m_send, m_recv, w_send, w_recv, f_send, f_recv, y_send, y_recv, x_send, x_recv,
 ):
     me = lax.axis_index("seq")
     req = lax.axis_index("req")
+    at_x, at_y = me // SIDE, lax.rem(me, SIDE)
+    core = lax.rem(req, 2)
     table_rows = NEW * HEADS
     lane = lax.broadcasted_iota(jnp.int32, (CHUNKS, LANES), 1)
 
@@ -125,10 +129,15 @@
 
     table_copy = local(table_hbm, table, 0)
     rel_copy = local(rel_hbm, rel, 1)
-    w_copy = local(w_hbm, w_qkv, 2)
-    out_copy = local(w_out_hbm, w_out, 3)
-    in_copy = local(w_in_hbm, w_in, 4)
-    down_copy = local(w_down_hbm, w_down, 5)
+    w_copies = [
+        local(
+            w_hbm.at[:, i * WIDTH : (i + 1) * WIDTH], w_qkv.at[:, i * WIDTH : (i + 1) * WIDTH], 2 + i
+        )
+        for i in range(3)
+    ]
+    out_copy = local(w_out_hbm, w_out, 5)
+    in_copy = local(w_in_hbm, w_ff.at[0, at_x], 6)
+    down_copy = local(w_down_hbm, w_ff.at[1, at_x], 7)
 
     def key_copy(r):
         return pltpu.make_async_copy(keys_hbm.at[r], keys.at[r], key_sems.at[r])
@@ -138,7 +147,8 @@
 
     table_copy.start()
     rel_copy.start()
-    w_copy.start()
+    w_copies[0].start()
+    w_copies[1].start()
     barrier = pltpu.get_barrier_semaphore()
     for k in range(1, SEQ_N):
         pl.semaphore_signal(
@@ -148,13 +158,17 @@
         pl.semaphore_signal(
             barrier, inc=1, device_id={"req": lax.rem(req + k, REQ_N)}, device_id_type=MESH
         )
-    for r in range(GROUP):
-        key_copy(r).start()
+    key_copy(0).start()
+    in_copy.start()
+    down_copy.start()
 
     vocab_rows = table.shape[0]
+    ids_pad[...] = jnp.zeros((8, LANES), jnp.int32)
+    ids_pad[0:NEW, 0 : REQ_N * GROUP] = ids_ref[...]
+    ids_t = ids_pad[...].T
     ids = jnp.concatenate(
         [
-            ids_ref[g * GROUP : (g + 1) * GROUP, t : t + 1]
+            ids_t[g * GROUP : (g + 1) * GROUP, t : t + 1]
             for g in range(REQ_N)
             for t in range(NEW)
         ],
@@ -189,11 +203,6 @@
 
     for copy in req_copies():
         copy.start()
-    for r in range(GROUP):
-        value_copy(r).start()
-    out_copy.start()
-    in_copy.start()
-    down_copy.start()
 
     rel_copy.wait()
     relative = layer_norm(rel[...].astype(f32), gain_ref[3:4, :], bias_ref[3:4, :]).astype(bf16)
@@ -203,10 +212,13 @@
         == BUCKETS - 1
     ).astype(f32).astype(bf16)
     flipped = jnp.dot(flip, relative, preferred_element_type=f32).astype(bf16)
-    w_copy.wait()
+    w_copies[0].wait()
     pos_lhs[...] = (
         jnp.dot(flipped, w_qkv[:, 0:WIDTH], preferred_element_type=f32).astype(bf16).T
     )
+    w_copies[1].wait()
+    key_copy(1).start()
+    w_copies[2].start()
     pos_key[...] = jnp.dot(
         relative, w_qkv[:, WIDTH : 2 * WIDTH], preferred_element_type=f32
     ).astype(bf16)
@@ -216,7 +228,52 @@
         col_head = lax.broadcasted_iota(jnp.int32, (NEW, HEADS, WIDTH), 2) >> 6
         return 2 * (row & (CHUNKS - 1)) + (row >> 3) == col_head
 
+    def near_copy(src, dst, send_sem, recv_sem, axis, peer):
+        return pltpu.make_async_remote_copy(
+            src_ref=src,
+            dst_ref=dst,
+            send_sem=send_sem,
+            recv_sem=recv_sem,
+            device_id={axis: peer},
+            device_id_type=MESH,
+        )
+
+    def x_peer(k):
+        return lax.rem(at_x + k, SIDE) * SIDE + at_y
+
+    def y_peer(k):
+        return at_x * SIDE + lax.rem(at_y + k, SIDE)
+
+    def shard_copies():
+        held = w_ff.at[core, at_x]
+        return [
+            near_copy(held, held, w_send.at[k], w_recv.at[k], "seq", x_peer(k))
+            for k in range(1, SIDE)
+        ]
+
+    def forward_copies():
+        copies = []
+        for k in range(1, SIDE):
+            held = w_ff.at[core, lax.rem(at_x + k, SIDE)]
+            copies.append(
+                near_copy(held, held, f_send.at[k], f_recv.at[k], "req", req + 1 - 2 * core)
+            )
+        return copies
+
     def from_pos_step(r, carry):
+        value_copy(r).start()
+
+        @pl.when(r < GROUP - 2)
+        def _():
+            key_copy(r + 2).start()
+
+        @pl.when(r == 0)
+        def _():
+            in_copy.wait()
+            down_copy.wait()
+            out_copy.start()
+            start_all(shard_copies())
+
         @pl.when(r == HOOKS[0])
         def _():
             copies = req_copies()
@@ -249,7 +306,11 @@
         def _():
             wait_all(seq_gather(me, hid.at[0], ag_send, ag_recv))
             stage[...] = hid[0].astype(f32).reshape(ROWS * CHUNKS, LANES)
-            hidden = tiles_to_rows(stage, ROWS).astype(bf16)
+            hidden = tiles_to_rows(stage, ROWS)
+            for one in range(SIDE):
+                h_zero[one] = hidden[one * 2 * NEW : (one + 1) * 2 * NEW, :]
+            hidden = hidden.astype(bf16)
+            w_copies[2].wait()
             projected = (
                 jnp.dot(hidden, w_qkv[...], preferred_element_type=f32).astype(bf16).astype(f32)
             )
@@ -287,13 +348,21 @@
 
     first = me * PIECE
 
-    def message_copy(r, pair):
-        peer = 2 * r + pair
-        return seq_copy(
-            msgs.at[peer], inbox.at[me], a_send.at[peer], a_recv.at[me], peer
-        )
+    def message_copies(r, k):
+        peer = (r // 2) * SIDE + k
+        slot = lax.rem(peer - me + SEQ_N, SEQ_N) - 1
+        part = lax.rem(r, 2)
+        return peer, [
+            near_copy(msg_numer.at[r], in_numer.at[slot, part], n_send, n_recv, "seq", peer),
+            near_copy(msg_ml.at[r], in_ml.at[slot, part], m_send, m_recv, "seq", peer),
+        ]
 
     def attend_step(r, carry):
+        @pl.when(r == FORWARD)
+        def _():
+            wait_all(shard_copies())
+            start_all(forward_copies())
+
         value_copy(r).wait()
         span = pl.ds(pl.multiple_of(r * table_rows, table_rows), table_rows)
         content = dot_nt(queries[span, :], keys[r])
@@ -340,133 +409,136 @@
         sums = jnp.sum(weights, axis=1, keepdims=True)
         wide = jnp.dot(weights.astype(bf16), values[r], preferred_element_type=f32)
         numer = jnp.sum(jnp.where(own_head(), wide.reshape(NEW, HEADS, WIDTH), 0.0), axis=1)
-        rows_to_tiles(numer, stage, NEW)
-        for pair in range(2):
-            peer = 2 * r + pair
-            msgs[peer, 0 : 2 * CHUNKS, :] = stage[
-                pair * 2 * CHUNKS : (pair + 1) * 2 * CHUNKS, :
-            ]
-            columns = []
-            for token in (2 * pair, 2 * pair + 1):
-                for j in range(2):
-                    at = token * HEADS + j * CHUNKS
-                    columns.append(top[at : at + CHUNKS])
-                    columns.append(sums[at : at + CHUNKS])
-            msgs[peer, 2 * CHUNKS : MSG, :] = pack_ml(columns, lane)
+        rows_to_tiles(numer, v_stage, NEW)
+        msg_numer[r] = v_stage[0 : NEW * CHUNKS, :].astype(bf16)
+        columns = []
+        for token in range(NEW):
+            for j in range(2):
+                at = token * HEADS + j * CHUNKS
+                columns.append(top[at : at + CHUNKS])
+                columns.append(sums[at : at + CHUNKS])
+        msg_ml[r] = pack_ml(columns, lane)
+        for k in range(SIDE):
+            peer, copies = message_copies(r, k)
 
             @pl.when(peer != me)
             def _():
-                message_copy(r, pair).start()
+                start_all(copies)
 
         return carry
 
     lax.fori_loop(0, GROUP, attend_step, 0)
 
-    odd = lax.rem(me, 2)
-    mine = proj[me // 2]
-    wanted = new_ref[me // 2]
-    for t in range(NEW):
-        picks[t * NEW : (t + 1) * NEW, :] = wanted[:, t : t + 1]
+    new_lane = lax.broadcasted_iota(jnp.int32, (NEW, NEW, GROUP), 2)
+    new_all = new_ref[...].astype(f32)
+    for i in range(2):
+        wanted = jnp.sum(
+            jnp.where(new_lane == 2 * at_x + i, new_all, 0.0), axis=2, keepdims=True
+        )
+        for t in range(NEW):
+            at = (i * NEW + t) * NEW
+            picks[at : at + NEW, :] = wanted[t]
     picked = (
-        lax.broadcasted_iota(jnp.int32, (NEW * NEW, BUCKETS), 1) == picks[...]
+        lax.broadcasted_iota(jnp.int32, (2 * NEW * NEW, BUCKETS), 1).astype(f32) == picks[...]
     ).astype(f32).astype(bf16)
     pq = dot_nt(picked, pos_lhs[...])
     pk = jnp.dot(picked, pos_key[...], preferred_element_type=f32)
-    q4, k4, v4 = (mine[:, i * WIDTH : (i + 1) * WIDTH] for i in range(3))
-    q16 = jnp.broadcast_to(q4[None], (NEW, NEW, WIDTH)).reshape(NEW * NEW, WIDTH)
-    k16 = jnp.broadcast_to(k4[:, None, :], (NEW, NEW, WIDTH)).reshape(NEW * NEW, WIDTH)
-    rows_to_tiles(q16 * (k16 + pk) + k16 * pq, fresh_stage, NEW * NEW)
-    rows_to_tiles(v4, stage, NEW)
-    columns = []
     for i in range(2):
-        token = 2 * odd + i
-        spread = []
-        for u in range(NEW):
-            at = pl.multiple_of((u * NEW + token) * CHUNKS, CHUNKS)
-            terms = fresh_stage[pl.ds(at, CHUNKS), :]
-            even = jnp.sum(jnp.where(lane < HEAD_DIM, terms, 0.0), axis=1, keepdims=True)
-            other = jnp.sum(jnp.where(lane >= HEAD_DIM, terms, 0.0), axis=1, keepdims=True)
-            spread.append(
-                jnp.where(u <= token, spread_pair(even, other, lane) * score_scale, masked_score)
+        mine = proj[2 * at_x + i]
+        q4, k4, v4 = (mine[:, w * WIDTH : (w + 1) * WIDTH] for w in range(3))
+        pairs = NEW * NEW
+        q16 = jnp.broadcast_to(q4[:, None, :], (NEW, NEW, WIDTH)).reshape(pairs, WIDTH)
+        k16 = jnp.broadcast_to(k4[None], (NEW, NEW, WIDTH)).reshape(pairs, WIDTH)
+        span = slice(i * pairs, (i + 1) * pairs)
+        rows_to_tiles(q16 * (k16 + pk[span]) + k16 * pq[span], fresh_stage, pairs)
+        rows_to_tiles(v4, v_stage, NEW)
+        columns = []
+        for t in range(NEW):
+            spread = []
+            for u in range(t + 1):
+                at = (t * NEW + u) * CHUNKS
+                terms = fresh_stage[at : at + CHUNKS, :]
+                even = jnp.sum(jnp.where(lane < HEAD_DIM, terms, 0.0), axis=1, keepdims=True)
+                other = jnp.sum(jnp.where(lane >= HEAD_DIM, terms, 0.0), axis=1, keepdims=True)
+                spread.append(spread_pair(even, other, lane) * score_scale)
+            top = functools.reduce(jnp.maximum, spread)
+            sums = jnp.zeros_like(top)
+            numer = jnp.zeros_like(top)
+            for u in range(t + 1):
+                weight = jnp.exp(spread[u] - top)
+                sums = sums + weight
+                numer = numer + weight.astype(bf16).astype(f32) * v_stage[
+                    u * CHUNKS : (u + 1) * CHUNKS, :
+                ]
+            fresh_numer[i, t * CHUNKS : (t + 1) * CHUNKS, :] = numer
+            for at in (0, HEAD_DIM):
+                columns.append(top[:, at : at + 1])
+                columns.append(sums[:, at : at + 1])
+        fresh_ml[i] = pack_ml(columns, lane)
+
+    near_copy(in_numer, in_numer, n_send, n_recv, "seq", x_peer(1)).wait()
+    near_copy(in_ml, in_ml, m_send, m_recv, "seq", x_peer(1)).wait()
+    for i in range(2):
+        mls = [in_ml[k, i] for k in range(SEQ_N - 1)] + [msg_ml[2 * at_x + i], fresh_ml[i]]
+        top = functools.reduce(jnp.maximum, mls)
+        factors = [jnp.exp(ml - top) for ml in mls]
+        denom = functools.reduce(
+            jnp.add, [f * pltpu.roll(ml, LANES - 8, axis=1) for f, ml in zip(factors, mls)]
+        )
+        numers = [jnp.zeros((CHUNKS, LANES), f32) for _ in range(NEW)]
+        for k, factor in enumerate(factors):
+            if k < SEQ_N - 1:
+                block = in_numer[k, i].astype(f32)
+            elif k == SEQ_N - 1:
+                block = msg_numer[2 * at_x + i].astype(f32)
+            else:
+                block = fresh_numer[i]
+            for t in range(NEW):
+                at = t * 32
+                numers[t] = numers[t] + block[t * CHUNKS : (t + 1) * CHUNKS] * spread_pair(
+                    factor[:, at : at + 1], factor[:, at + 16 : at + 17], lane
+                )
+        for t in range(NEW):
+            at = t * 32
+            row = (i * NEW + t) * CHUNKS
+            att[row : row + CHUNKS, :] = numers[t] / spread_pair(
+                denom[:, at : at + 1], denom[:, at + 16 : at + 17], lane
             )
-        top = functools.reduce(jnp.maximum, spread)
-        sums = jnp.zeros_like(top)
-        numer = jnp.zeros_like(top)
-        for u in range(NEW):
-            weight = jnp.where(u <= token, jnp.exp(spread[u] - top), 0.0)
-            sums = sums + weight
-            numer = numer + weight.astype(bf16).astype(f32) * stage[
-                u * CHUNKS : (u + 1) * CHUNKS, :
-            ]
-        fresh[i * CHUNKS : (i + 1) * CHUNKS, :] = numer
-        for at in (0, HEAD_DIM):
-            columns.append(top[:, at : at + 1])
-            columns.append(sums[:, at : at + 1])
-    fresh[2 * CHUNKS : MSG, :] = pack_ml(columns, lane)
-
-    inbox[me] = msgs[me]
-    for k in range(1, SEQ_N):
-        peer = lax.rem(me + k, SEQ_N)
-        seq_copy(
-            msgs.at[peer], inbox.at[peer], a_send.at[peer], a_recv.at[peer], peer
-        ).wait()
-    sources = [inbox.at[k] for k in range(SEQ_N)] + [fresh]
-    for i in range(2):
-        tops, sums = [], []
-        for source in sources:
-            ml = source[2 * CHUNKS : MSG, :]
-            at = i * HEAD_DIM
-            tops.append(spread_pair(ml[:, at : at + 1], ml[:, at + 32 : at + 33], lane))
-            sums.append(spread_pair(ml[:, at + 16 : at + 17], ml[:, at + 48 : at + 49], lane))
-        top = functools.reduce(jnp.maximum, tops)
-        numer = jnp.zeros_like(top)
-        denom = jnp.zeros_like(top)
-        for source, one, part in zip(sources, tops, sums):
-            factor = jnp.exp(one - top)
-            numer = numer + factor * source[i * CHUNKS : (i + 1) * CHUNKS, :]
-            denom = denom + factor * part
-        rows_f[i * CHUNKS : (i + 1) * CHUNKS, :] = numer / denom
-    attended = tiles_to_rows(rows_f, 2).astype(bf16)
-    rows_f[...] = hid[0, me].astype(f32)
-    hidden_zero = tiles_to_rows(rows_f, 2)
+    attended = tiles_to_rows(att, 2 * NEW).astype(bf16)
     out_copy.wait()
     attn_out = jnp.dot(attended, w_out[...], preferred_element_type=f32)
-    hidden_one = (
-        layer_norm(hidden_zero + attn_out, gain_ref[1:2, :], bias_ref[1:2, :])
-        .astype(bf16)
-        .astype(f32)
-    )
-    rows_to_tiles(hidden_one, rows_f, 2)
-    hid[1, me] = rows_f[...].astype(bf16)
-    copies = seq_gather(me, hid.at[1], b_send, b_recv)
-    start_all(copies)
-    in_copy.wait()
-    down_copy.wait()
-    wait_all(copies)
-    stage[...] = hid[1].astype(f32).reshape(ROWS * CHUNKS, LANES)
-    everyone = tiles_to_rows(stage, ROWS).astype(bf16)
-    inner = dot_nt(everyone, w_in[...])
-    inner = (0.5 * inner * (1.0 + lax.erf(inner * math.sqrt(0.5)))).astype(bf16)
-    rows_to_tiles(jnp.dot(inner, w_down[...], preferred_element_type=f32), stage, ROWS)
-    tiles[1] = stage[...].reshape(SEQ_N, 2 * CHUNKS, LANES).astype(bf16)
-    copies = seq_scatter(me, tiles.at[1], got.at[1], c_send, c_recv)
-    start_all(copies)
-    total = tiles[1, me].astype(f32)
-    for k in range(1, SEQ_N):
-        copies[k - 1].wait()
-        total = total + got[1, k].astype(f32)
-    rows_f[...] = total
-    mlp_out = tiles_to_rows(rows_f, 2)
-    layer_out = layer_norm(hidden_one + mlp_out, gain_ref[2:3, :], bias_ref[2:3, :])
-    rows_to_tiles(layer_out, rows_f, 2)
-    hid[2, me] = rows_f[...].astype(bf16)
-    copies = seq_gather(me, hid.at[2], d_send, d_recv)
+    hidden_one = layer_norm(
+        h_zero[at_x] + attn_out, gain_ref[1:2, :], bias_ref[1:2, :]
+    ).astype(bf16)
+    wait_all(forward_copies())
+    total = jnp.zeros((2 * NEW, WIDTH), f32)
+    for one in range(SIDE):
+        inner = dot_nt(hidden_one, w_ff[0, one])
+        inner = (0.5 * inner * (1.0 + lax.erf(inner * math.sqrt(0.5)))).astype(bf16)
+        total = total + jnp.dot(inner, w_ff[1, one], preferred_element_type=f32)
+    partial[at_y] = total.astype(bf16)
+    copies = [
+        near_copy(
+            partial.at[at_y], partial.at[at_y], y_send.at[k], y_recv.at[k], "seq", y_peer(k)
+        )
+        for k in range(1, SIDE)
+    ]
     start_all(copies)
     wait_all(copies)
-    stage[...] = hid[2].astype(f32).reshape(ROWS * CHUNKS, LANES)
-    everyone = tiles_to_rows(stage, ROWS)
-    for r in range(GROUP):
-        out_ref[r] = everyone[r * NEW : (r + 1) * NEW, :].astype(bf16)
+    mlp_out = functools.reduce(jnp.add, [partial[k].astype(f32) for k in range(SIDE)])
+    final[at_x] = layer_norm(
+        hidden_one.astype(f32) + mlp_out, gain_ref[2:3, :], bias_ref[2:3, :]
+    ).astype(bf16)
+    copies = [
+        near_copy(final.at[at_x], final.at[at_x], x_send.at[k], x_recv.at[k], "seq", x_peer(k))
+        for k in range(1, SIDE)
+    ]
+    start_all(copies)
+    wait_all(copies)
+    for one in range(SIDE):
+        rows = final[one].astype(f32)
+        for i in range(2):
+            out_ref[2 * one + i] = rows[i * NEW : (i + 1) * NEW, :].astype(bf16)
 
 
 def shards(
@@ -505,15 +577,17 @@
             pltpu.VMEM(w_out.shape, bf16),
             pltpu.VMEM(cache_keys.shape, bf16),
             pltpu.VMEM(cache_values.shape, bf16),
-            pltpu.VMEM(w_in.shape, bf16),
-            pltpu.VMEM(w_down.shape, bf16),
+            pltpu.VMEM((2, SIDE) + w_in.shape, bf16),
+            pltpu.VMEM((8, LANES), jnp.int32),
             pltpu.VMEM((REQ_N, ROWS, WIDTH), bf16),
             pltpu.VMEM((REQ_N, ROWS, WIDTH), bf16),
             pltpu.VMEM((ROWS * CHUNKS, LANES), f32),
-            pltpu.VMEM((2,) + slot, bf16),
-            pltpu.VMEM((2,) + slot, bf16),
-            pltpu.VMEM((3,) + slot, bf16),
+            pltpu.VMEM((1,) + slot, bf16),
+            pltpu.VMEM((1,) + slot, bf16),
+            pltpu.VMEM((1,) + slot, bf16),
+            pltpu.VMEM((SIDE, 2 * NEW, WIDTH), f32),
             pltpu.VMEM((2 * CHUNKS, LANES), f32),
+            pltpu.VMEM((2 * NEW * CHUNKS, LANES), f32),
             pltpu.VMEM((GROUP, NEW, 3 * WIDTH), f32),
             pltpu.VMEM((WIDTH, BUCKETS), bf16),
             pltpu.VMEM((BUCKETS, WIDTH), bf16),
@@ -521,24 +595,33 @@
             pltpu.VMEM((GROUP, PIECE // LANES * NEW * HEADS, LANES), f32),
             pltpu.VMEM((GROUP * NEW * HEADS, WIDTH), bf16),
             pltpu.VMEM((GROUP * NEW * HEADS, BUCKETS), f32),
-            pltpu.VMEM((SEQ_N, MSG, LANES), f32),
-            pltpu.VMEM((SEQ_N, MSG, LANES), f32),
-            pltpu.VMEM((MSG, LANES), f32),
+            pltpu.VMEM((GROUP, NEW * CHUNKS, LANES), bf16),
+            pltpu.VMEM((GROUP, CHUNKS, LANES), f32),
+            pltpu.VMEM((SEQ_N - 1, 2, NEW * CHUNKS, LANES), bf16),
+            pltpu.VMEM((SEQ_N - 1, 2, CHUNKS, LANES), f32),
+            pltpu.VMEM((2, NEW * CHUNKS, LANES), f32),
+            pltpu.VMEM((2, CHUNKS, LANES), f32),
             pltpu.VMEM((NEW * NEW * CHUNKS, LANES), f32),
-            pltpu.VMEM((NEW * NEW, 1), jnp.int32),
-            pltpu.SemaphoreType.DMA((6,)),
+            pltpu.VMEM((NEW * CHUNKS, LANES), f32),
+            pltpu.VMEM((2 * NEW * NEW, 1), f32),
+            pltpu.VMEM((SIDE, 2 * NEW, WIDTH), bf16),
+            pltpu.VMEM((SIDE, 2 * NEW, WIDTH), bf16),
+            pltpu.SemaphoreType.DMA((8,)),
             pltpu.SemaphoreType.DMA((GROUP,)),
             pltpu.SemaphoreType.DMA((GROUP,)),
         ]
         + [pltpu.SemaphoreType.DMA((REQ_N,))] * 2
-        + [pltpu.SemaphoreType.DMA((SEQ_N,))] * 12,
+        + [pltpu.SemaphoreType.DMA((SEQ_N,))] * 4
+        + [pltpu.SemaphoreType.DMA] * 4
+        + [pltpu.SemaphoreType.DMA((SIDE,))] * 8,
         compiler_params=pltpu.CompilerParams(
             collective_id=0, has_side_effects=True, vmem_limit_bytes=60 << 20
         ),
         name="decode_layer",
     )(
-        token_ids, embed_table, ln_gains, ln_biases, rel_table, w_qkv, w_out, cache_keys,
-        cache_values, lengths, window_starts, cache_buckets, new_buckets, w_in, w_down,
+        token_ids.T, embed_table, ln_gains, ln_biases, rel_table, w_qkv, w_out, cache_keys,
+        cache_values, lengths, window_starts, cache_buckets,
+        jnp.transpose(new_buckets, (1, 2, 0)), w_in, w_down,
     )
 
 

time: 72.6 us -> 74.6 us (1.028)
  Pallas kernels: 68 us -> 72.9 us
  local copies, waits for them, and re-layouts: 4.26 us -> 1.49 us
    pallas_call x1, Pallas kernels: 68 us -> 72.9 us  [shards(): pl.pallas_call(layer_kernel, out_shape=jax.ShapeDtypeStruct((GROUP, NEW,...]
    unnamed x3 -> x1, local copies, waits for them, and re-layouts: 4.26 us -> 1.49 us
where the time goes in v3:
time: 74.6 us; the launch traced here: 74.4 us
  Pallas kernels  72.9 us (98%)
  local copies, waits for them, and re-layouts  1.49 us (2%)
    pallas_call x1, Pallas kernels, shards(): pl.pallas_call(layer_kernel, out_shape=jax.ShapeDtypeStruct((GROUP, NEW,...  72.9 us
    unnamed x1, local copies, waits for them, and re-layouts  1.49 us

profile of v3, /device:TPU:0, one launch (start us, length us, event | category | flops | bytes accessed | tf_op | source)
XLA Modules:
  0.0 74.4 jit_solution(5228047580707403974)
XLA Ops:
  0.0 72.9 %decode_layer.1 = bf16[8,4,1024]{2,1,0:T(4,128)(2,1)} custom-call(s32[4,64]{1,0:T(4,128)} %bitcast.3, bf16[1000,1024]{1,0:T(8,128)(2,1)} %table_hbm.1, f32[4,1024]{1,0:T(4,128)} %gain_ref.1, f32[4,1024]{1,0:T(4,128)} %bias_ref.1, bf16[512,1024]{1,0:T(8,128)(2,1)} %rel_hbm.1, bf16[1024,3072]{1,0:T(8,128)(2,1)} %w_hbm.1, bf16[1024,1024]{1,0:T(8,128)(2,1)} %w_out_hbm.1, ...), custom_call_target="tpu_custom_call" | custom-call | tf_op jit(solution)/shard_map/decode_layer/pallas_call | solution.py:565
  72.9 1.5 %copy.17 = bf16[8,4,1024]{2,1,0:T(4,128)(2,1)} copy(bf16[8,4,1024]{2,1,0:T(4,128)(2,1)} %decode_layer.1) | data formatting | bytes 131072

commit v4 on v3

--- a/solution.py
+++ b/solution.py
@@ -24,7 +24,7 @@
 CHUNKS = WIDTH // LANES
 SIDE = 4
 HOOKS = (3, 5, 7)
-FORWARD = 4
+FORWARD = 0
 
 norm_epsilon = 1e-06
 masked_score = -1e30
@@ -204,6 +204,54 @@
     for copy in req_copies():
         copy.start()
 
+    def near_copy(src, dst, send_sem, recv_sem, axis, peer):
+        return pltpu.make_async_remote_copy(
+            src_ref=src,
+            dst_ref=dst,
+            send_sem=send_sem,
+            recv_sem=recv_sem,
+            device_id={axis: peer},
+            device_id_type=MESH,
+        )
+
+    def x_slot(k):
+        return lax.rem(at_x + k, SIDE)
+
+    def x_peer(k):
+        return x_slot(k) * SIDE + at_y
+
+    def y_peer(k):
+        return at_x * SIDE + lax.rem(at_y + k, SIDE)
+
+    def shard_copies():
+        held = w_ff.at[core, at_x]
+        return [
+            near_copy(held, held, w_send.at[k], w_recv.at[k], "seq", x_peer(k)) for k in (1, 3)
+        ]
+
+    def far_copies():
+        half = w_ff.shape[2] // 2
+        copies = []
+        for index, (k, rows) in enumerate(((1, slice(0, half)), (3, slice(half, 2 * half)))):
+            held = w_ff.at[core, x_slot(k + 2), rows]
+            copies.append(
+                near_copy(held, held, w_send.at[2 * index], w_recv.at[2 * index], "seq", x_peer(k))
+            )
+        return copies
+
+    def forward_copies(offsets):
+        copies = []
+        for k in offsets:
+            held = w_ff.at[core, x_slot(k)]
+            copies.append(
+                near_copy(held, held, f_send.at[k], f_recv.at[k], "req", req + 1 - 2 * core)
+            )
+        return copies
+
+    in_copy.wait()
+    down_copy.wait()
+    start_all(shard_copies())
+
     rel_copy.wait()
     relative = layer_norm(rel[...].astype(f32), gain_ref[3:4, :], bias_ref[3:4, :]).astype(bf16)
     flip = (
@@ -228,38 +276,6 @@
         col_head = lax.broadcasted_iota(jnp.int32, (NEW, HEADS, WIDTH), 2) >> 6
         return 2 * (row & (CHUNKS - 1)) + (row >> 3) == col_head
 
-    def near_copy(src, dst, send_sem, recv_sem, axis, peer):
-        return pltpu.make_async_remote_copy(
-            src_ref=src,
-            dst_ref=dst,
-            send_sem=send_sem,
-            recv_sem=recv_sem,
-            device_id={axis: peer},
-            device_id_type=MESH,
-        )
-
-    def x_peer(k):
-        return lax.rem(at_x + k, SIDE) * SIDE + at_y
-
-    def y_peer(k):
-        return at_x * SIDE + lax.rem(at_y + k, SIDE)
-
-    def shard_copies():
-        held = w_ff.at[core, at_x]
-        return [
-            near_copy(held, held, w_send.at[k], w_recv.at[k], "seq", x_peer(k))
-            for k in range(1, SIDE)
-        ]
-
-    def forward_copies():
-        copies = []
-        for k in range(1, SIDE):
-            held = w_ff.at[core, lax.rem(at_x + k, SIDE)]
-            copies.append(
-                near_copy(held, held, f_send.at[k], f_recv.at[k], "req", req + 1 - 2 * core)
-            )
-        return copies
-
     def from_pos_step(r, carry):
         value_copy(r).start()
 
@@ -269,10 +285,7 @@
 
         @pl.when(r == 0)
         def _():
-            in_copy.wait()
-            down_copy.wait()
             out_copy.start()
-            start_all(shard_copies())
 
         @pl.when(r == HOOKS[0])
         def _():
@@ -361,7 +374,8 @@
         @pl.when(r == FORWARD)
         def _():
             wait_all(shard_copies())
-            start_all(forward_copies())
+            start_all(far_copies())
+            start_all(forward_copies((1, 3)))
 
         value_copy(r).wait()
         span = pl.ds(pl.multiple_of(r * table_rows, table_rows), table_rows)
@@ -428,6 +442,9 @@
         return carry
 
     lax.fori_loop(0, GROUP, attend_step, 0)
+
+    wait_all(far_copies())
+    start_all(forward_copies((2,)))
 
     new_lane = lax.broadcasted_iota(jnp.int32, (NEW, NEW, GROUP), 2)
     new_all = new_ref[...].astype(f32)
@@ -510,7 +527,7 @@
     hidden_one = layer_norm(
         h_zero[at_x] + attn_out, gain_ref[1:2, :], bias_ref[1:2, :]
     ).astype(bf16)
-    wait_all(forward_copies())
+    wait_all(forward_copies((1, 2, 3)))
     total = jnp.zeros((2 * NEW, WIDTH), f32)
     for one in range(SIDE):
         inner = dot_nt(hidden_one, w_ff[0, one])

time: 74.6 us -> 60.2 us (0.81)
  Pallas kernels: 72.9 us -> 58.5 us
    pallas_call x1, Pallas kernels: 72.9 us -> 58.5 us  [shards(): pl.pallas_call(layer_kernel, out_shape=jax.ShapeDtypeStruct((GROUP, NEW,...]
where the time goes in v4:
time: 60.2 us; the launch traced here: 60 us
  Pallas kernels  58.5 us (97%)
  local copies, waits for them, and re-layouts  1.49 us (2%)
    pallas_call x1, Pallas kernels, shards(): pl.pallas_call(layer_kernel, out_shape=jax.ShapeDtypeStruct((GROUP, NEW,...  58.5 us
    unnamed x1, local copies, waits for them, and re-layouts  1.49 us

profile of v4, /device:TPU:0, one launch (start us, length us, event | category | flops | bytes accessed | tf_op | source)
XLA Modules:
  0.0 60.0 jit_solution(5157439503018587098)
XLA Ops:
  0.0 58.5 %decode_layer.1 = bf16[8,4,1024]{2,1,0:T(4,128)(2,1)} custom-call(s32[4,64]{1,0:T(4,128)} %bitcast.3, bf16[1000,1024]{1,0:T(8,128)(2,1)} %table_hbm.1, f32[4,1024]{1,0:T(4,128)} %gain_ref.1, f32[4,1024]{1,0:T(4,128)} %bias_ref.1, bf16[512,1024]{1,0:T(8,128)(2,1)} %rel_hbm.1, bf16[1024,3072]{1,0:T(8,128)(2,1)} %w_hbm.1, bf16[1024,1024]{1,0:T(8,128)(2,1)} %w_out_hbm.1, ...), custom_call_target="tpu_custom_call" | custom-call | tf_op jit(solution)/shard_map/decode_layer/pallas_call | solution.py:582
  58.5 1.5 %copy.17 = bf16[8,4,1024]{2,1,0:T(4,128)(2,1)} copy(bf16[8,4,1024]{2,1,0:T(4,128)(2,1)} %decode_layer.1) | data formatting | bytes 131072

commit v5 on v4

--- a/solution.py
+++ b/solution.py
@@ -24,7 +24,8 @@
 CHUNKS = WIDTH // LANES
 SIDE = 4
 HOOKS = (3, 5, 7)
-FORWARD = 0
+PASS_ON = 6
+FORWARD = 6
 
 norm_epsilon = 1e-06
 masked_score = -1e30
@@ -183,6 +184,14 @@
         .astype(bf16)
         .reshape(REQ_N, ROWS, WIDTH)
     )
+    rel_copy.wait()
+    relative = layer_norm(rel[...].astype(f32), gain_ref[3:4, :], bias_ref[3:4, :]).astype(bf16)
+    flip = (
+        lax.broadcasted_iota(jnp.int32, (BUCKETS, BUCKETS), 0)
+        + lax.broadcasted_iota(jnp.int32, (BUCKETS, BUCKETS), 1)
+        == BUCKETS - 1
+    ).astype(f32).astype(bf16)
+    flipped = jnp.dot(flip, relative, preferred_element_type=f32).astype(bf16)
     pl.semaphore_wait(barrier, SEQ_N - 1 + REQ_N - 1)
 
     def req_copies():
@@ -252,14 +261,6 @@
     down_copy.wait()
     start_all(shard_copies())
 
-    rel_copy.wait()
-    relative = layer_norm(rel[...].astype(f32), gain_ref[3:4, :], bias_ref[3:4, :]).astype(bf16)
-    flip = (
-        lax.broadcasted_iota(jnp.int32, (BUCKETS, BUCKETS), 0)
-        + lax.broadcasted_iota(jnp.int32, (BUCKETS, BUCKETS), 1)
-        == BUCKETS - 1
-    ).astype(f32).astype(bf16)
-    flipped = jnp.dot(flip, relative, preferred_element_type=f32).astype(bf16)
     w_copies[0].wait()
     pos_lhs[...] = (
         jnp.dot(flipped, w_qkv[:, 0:WIDTH], preferred_element_type=f32).astype(bf16).T
@@ -286,6 +287,12 @@
         @pl.when(r == 0)
         def _():
             out_copy.start()
+
+        @pl.when(r == PASS_ON)
+        def _():
+            wait_all(shard_copies())
+            start_all(far_copies())
+            start_all(forward_copies((1, 3)))
 
         @pl.when(r == HOOKS[0])
         def _():
@@ -370,12 +377,13 @@
             near_copy(msg_ml.at[r], in_ml.at[slot, part], m_send, m_recv, "seq", peer),
         ]
 
-    def attend_step(r, carry):
-        @pl.when(r == FORWARD)
+    def attend_step(step, carry):
+        r = 2 * x_slot(step // 2 + 1) + lax.rem(step, 2)
+
+        @pl.when(step == FORWARD)
         def _():
-            wait_all(shard_copies())
-            start_all(far_copies())
-            start_all(forward_copies((1, 3)))
+            wait_all(far_copies())
+            start_all(forward_copies((2,)))
 
         value_copy(r).wait()
         span = pl.ds(pl.multiple_of(r * table_rows, table_rows), table_rows)
@@ -442,9 +450,6 @@
         return carry
 
     lax.fori_loop(0, GROUP, attend_step, 0)
-
-    wait_all(far_copies())
-    start_all(forward_copies((2,)))
 
     new_lane = lax.broadcasted_iota(jnp.int32, (NEW, NEW, GROUP), 2)
     new_all = new_ref[...].astype(f32)

time: 60.2 us -> 57.1 us (0.949)
  Pallas kernels: 58.5 us -> 55.4 us
    pallas_call x1, Pallas kernels: 58.5 us -> 55.4 us  [shards(): pl.pallas_call(layer_kernel, out_shape=jax.ShapeDtypeStruct((GROUP, NEW,...]
where the time goes in v5:
time: 57.1 us; the launch traced here: 56.9 us
  Pallas kernels  55.4 us (97%)
  local copies, waits for them, and re-layouts  1.49 us (3%)
    pallas_call x1, Pallas kernels, shards(): pl.pallas_call(layer_kernel, out_shape=jax.ShapeDtypeStruct((GROUP, NEW,...  55.4 us
    unnamed x1, local copies, waits for them, and re-layouts  1.49 us

profile of v5, /device:TPU:0, one launch (start us, length us, event | category | flops | bytes accessed | tf_op | source)
XLA Modules:
  0.0 56.9 jit_solution(17214664611401827526)
XLA Ops:
  0.0 55.4 %decode_layer.1 = bf16[8,4,1024]{2,1,0:T(4,128)(2,1)} custom-call(s32[4,64]{1,0:T(4,128)} %bitcast.3, bf16[1000,1024]{1,0:T(8,128)(2,1)} %table_hbm.1, f32[4,1024]{1,0:T(4,128)} %gain_ref.1, f32[4,1024]{1,0:T(4,128)} %bias_ref.1, bf16[512,1024]{1,0:T(8,128)(2,1)} %rel_hbm.1, bf16[1024,3072]{1,0:T(8,128)(2,1)} %w_hbm.1, bf16[1024,1024]{1,0:T(8,128)(2,1)} %w_out_hbm.1, ...), custom_call_target="tpu_custom_call" | custom-call | tf_op jit(solution)/shard_map/decode_layer/pallas_call | solution.py:587
  55.4 1.5 %copy.17 = bf16[8,4,1024]{2,1,0:T(4,128)(2,1)} copy(bf16[8,4,1024]{2,1,0:T(4,128)(2,1)} %decode_layer.1) | data formatting | bytes 131072

commit v6 on v5

--- a/solution.py
+++ b/solution.py
@@ -146,6 +146,8 @@
     def value_copy(r):
         return pltpu.make_async_copy(values_hbm.at[r], values.at[r], value_sems.at[r])
 
+    in_copy.start()
+    down_copy.start()
     table_copy.start()
     rel_copy.start()
     w_copies[0].start()
@@ -160,8 +162,6 @@
             barrier, inc=1, device_id={"req": lax.rem(req + k, REQ_N)}, device_id_type=MESH
         )
     key_copy(0).start()
-    in_copy.start()
-    down_copy.start()
 
     vocab_rows = table.shape[0]
     ids_pad[...] = jnp.zeros((8, LANES), jnp.int32)
@@ -186,12 +186,6 @@
     )
     rel_copy.wait()
     relative = layer_norm(rel[...].astype(f32), gain_ref[3:4, :], bias_ref[3:4, :]).astype(bf16)
-    flip = (
-        lax.broadcasted_iota(jnp.int32, (BUCKETS, BUCKETS), 0)
-        + lax.broadcasted_iota(jnp.int32, (BUCKETS, BUCKETS), 1)
-        == BUCKETS - 1
-    ).astype(f32).astype(bf16)
-    flipped = jnp.dot(flip, relative, preferred_element_type=f32).astype(bf16)
     pl.semaphore_wait(barrier, SEQ_N - 1 + REQ_N - 1)
 
     def req_copies():
@@ -263,7 +257,7 @@
 
     w_copies[0].wait()
     pos_lhs[...] = (
-        jnp.dot(flipped, w_qkv[:, 0:WIDTH], preferred_element_type=f32).astype(bf16).T
+        jnp.dot(relative, w_qkv[:, 0:WIDTH], preferred_element_type=f32).astype(bf16).T
     )
     w_copies[1].wait()
     key_copy(1).start()
@@ -351,7 +345,7 @@
                 cols = slice(half * TILE, (half + 1) * TILE)
                 chosen = (
                     lax.broadcasted_iota(jnp.int32, (BUCKETS, TILE), 0)
-                    == buckets_ref[r, t : t + 1, cols]
+                    == BUCKETS - 1 - buckets_ref[r, t : t + 1, cols]
                 ).astype(f32).astype(bf16)
                 product = (
                     jnp.dot(pos_lhs[...], chosen, preferred_element_type=f32) * keys_t[:, cols]
@@ -460,10 +454,10 @@
         for t in range(NEW):
             at = (i * NEW + t) * NEW
             picks[at : at + NEW, :] = wanted[t]
-    picked = (
-        lax.broadcasted_iota(jnp.int32, (2 * NEW * NEW, BUCKETS), 1).astype(f32) == picks[...]
-    ).astype(f32).astype(bf16)
-    pq = dot_nt(picked, pos_lhs[...])
+    buckets = lax.broadcasted_iota(jnp.int32, (2 * NEW * NEW, BUCKETS), 1).astype(f32)
+    picked = (buckets == picks[...]).astype(f32).astype(bf16)
+    mirrored = (buckets == BUCKETS - 1 - picks[...]).astype(f32).astype(bf16)
+    pq = dot_nt(mirrored, pos_lhs[...])
     pk = jnp.dot(picked, pos_key[...], preferred_element_type=f32)
     for i in range(2):
         mine = proj[2 * at_x + i]

time: 57.1 us -> 57.1 us (level)
  no operation moved by 1% of the time
where the time goes in v6:
time: 57.1 us; the launch traced here: 56.9 us
  Pallas kernels  55.4 us (97%)
  local copies, waits for them, and re-layouts  1.49 us (3%)
    pallas_call x1, Pallas kernels, shards(): pl.pallas_call(layer_kernel, out_shape=jax.ShapeDtypeStruct((GROUP, NEW,...  55.4 us
    unnamed x1, local copies, waits for them, and re-layouts  1.49 us

profile of v6, /device:TPU:0, one launch (start us, length us, event | category | flops | bytes accessed | tf_op | source)
XLA Modules:
  0.0 56.9 jit_solution(14897888267280381235)
XLA Ops:
  0.0 55.4 %decode_layer.1 = bf16[8,4,1024]{2,1,0:T(4,128)(2,1)} custom-call(s32[4,64]{1,0:T(4,128)} %bitcast.3, bf16[1000,1024]{1,0:T(8,128)(2,1)} %table_hbm.1, f32[4,1024]{1,0:T(4,128)} %gain_ref.1, f32[4,1024]{1,0:T(4,128)} %bias_ref.1, bf16[512,1024]{1,0:T(8,128)(2,1)} %rel_hbm.1, bf16[1024,3072]{1,0:T(8,128)(2,1)} %w_hbm.1, bf16[1024,1024]{1,0:T(8,128)(2,1)} %w_out_hbm.1, ...), custom_call_target="tpu_custom_call" | custom-call | tf_op jit(solution)/shard_map/decode_layer/pallas_call | solution.py:581
  55.4 1.5 %copy.17 = bf16[8,4,1024]{2,1,0:T(4,128)(2,1)} copy(bf16[8,4,1024]{2,1,0:T(4,128)(2,1)} %decode_layer.1) | data formatting | bytes 131072
